TPU v7x, 32 devices: a whole 2x2x4 slice. The times are simulated.
32 devices in a mesh: row: 4 (over y, core), col: 8 (over z, x).
Axes of the slice: x: 2, y: 2, z: 4, core: 2. Of those that a mesh axis runs over, the one named last changes fastest.
Arguments:
- patches: float32 [32, 64, 2, 128, 128], P('row', 'col'), may hold values from -6 to 6
- right_offset: int32 [32, 64], P('row', 'col'), may hold values from 57 to 112, as said below
- right_width: int32 [32, 64], P('row', 'col'), may hold values from 16 to 64
- down_offset: int32 [32, 64], P('row', 'col'), may hold values from 57 to 112, as said below
- down_width: int32 [32, 64], P('row', 'col'), may hold values from 16 to 64
Outputs:
- blended: float32 [32, 64, 2, 128, 128], P('row', 'col')
- phases: float32 [2, 32, 64], P(None, 'row', 'col')
Inputs may be any that keep to these rules, and one draw needn't show every extreme that they name: right_offset + right_width lies above 120 and at most 128. down_offset + down_width lies above 120 and at most 128.
All inputs are finite; a program needn't handle non-finite values.
Results may differ from a plain program's by a relative error of at most 0.0003.
Values sent between devices are 32-bit elements; how exact they have to be, the bound alone decides.
A program may use at most 128 MiB of HBM per device.

v0:
```python
import jax
import jax.numpy as jnp
from jax import lax
from jax.sharding import PartitionSpec as P

ITERS = 2


eps_norm = 1.0
highest = lax.Precision.HIGHEST


def extended(array, sides, width):
    for axis, dim in sides:
        size, length = (lax.axis_size(axis), array.shape[dim])
        up = [(i, (i + 1) % size) for i in range(size - 1)]
        down = [(j, i) for i, j in up]
        last = lax.slice_in_dim(array, length - width, length, axis=dim)
        first = lax.slice_in_dim(array, 0, width, axis=dim)
        before = lax.ppermute(last, axis, up)
        after = lax.ppermute(first, axis, down)
        array = jnp.concatenate([before, array, after], axis=dim)
    return array


def shifted_2(array, axis, by):
    size = lax.axis_size(axis)
    pairs = [(i, i + by) for i in range(size) if 0 <= i + by < size]
    return lax.ppermute(array, axis, pairs)


def correlate(shifted, partner, width_table):
    real_part = jnp.sum(
        shifted[..., 0, :, :] * partner[..., 0, :, :]
        + shifted[..., 1, :, :] * partner[..., 1, :, :],
        axis=(-2, -1),
    )
    imag_part = jnp.sum(
        shifted[..., 0, :, :] * partner[..., 1, :, :]
        - shifted[..., 1, :, :] * partner[..., 0, :, :],
        axis=(-2, -1),
    )
    scale = 1.0 / jnp.sqrt(partner.shape[-1] * width_table.astype(jnp.float32))
    return jnp.stack([real_part * scale, imag_part * scale])


def complex_times(factor, field):
    return jnp.stack(
        [factor[0] * field[0] - factor[1] * field[1], factor[0] * field[1] + factor[1] * field[0]]
    )


def conj_times(factor, field):
    return jnp.stack(
        [factor[0] * field[0] + factor[1] * field[1], factor[0] * field[1] - factor[1] * field[0]]
    )


def rotate(factor, field):
    real_part = (
        factor[..., 0:1, :, :] * field[..., 0:1, :, :]
        - factor[..., 1:2, :, :] * field[..., 1:2, :, :]
    )
    imag_part = (
        factor[..., 0:1, :, :] * field[..., 1:2, :, :]
        + factor[..., 1:2, :, :] * field[..., 0:1, :, :]
    )
    return jnp.concatenate([real_part, imag_part], axis=-3)


def neighbours(phase_now):
    padded = extended(phase_now, (("row", 1), ("col", 2)), 1)
    return (padded[:, 1:-1, 2:], padded[:, 2:, 1:-1], padded[:, 1:-1, :-2], padded[:, :-2, 1:-1])


def apply_sync(phase_now, corr_east, corr_south, corr_west, corr_north):
    east_phase, south_phase, west_phase, north_phase = neighbours(phase_now)
    image = complex_times(corr_east, east_phase) + complex_times(corr_south, south_phase)
    return image + conj_times(corr_west, west_phase) + conj_times(corr_north, north_phase)


def scale_last(square_sums, count):
    totals = lax.psum(jnp.stack(square_sums), ("row", "col"))
    factor = jnp.ones((), jnp.float32)
    for step in range(len(square_sums)):
        factor = factor / jnp.sqrt(factor * factor * totals[step] / count + eps_norm)
    return factor


def local(patches, right_offset, right_width, down_offset, down_width):
    rows_here = patches.shape[0]
    cols_here = patches.shape[1]
    patch_side = patches.shape[3]
    lane_index = jnp.arange(patch_side, dtype=jnp.int32)
    east_edge = shifted_2(patches[:, 0:1], "col", -1)
    south_edge = shifted_2(patches[0:1], "row", -1)
    east_patch = jnp.concatenate([patches[:, 1:], east_edge], axis=1)
    south_patch = jnp.concatenate([patches[1:], south_edge], axis=0)
    east_select = (
        (lane_index[:, None] == lane_index[None, :] + right_offset[:, :, None, None])
        & (lane_index[None, :] < right_width[:, :, None, None])
    ).astype(jnp.float32)
    south_select = (
        (lane_index[:, None] == lane_index[None, :] + down_offset[:, :, None, None])
        & (lane_index[None, :] < down_width[:, :, None, None])
    ).astype(jnp.float32)
    east_shifted = jnp.einsum("pqkrc,pqcd->pqkrd", patches, east_select, precision=highest)
    south_shifted = jnp.einsum("pqab,pqkac->pqkbc", south_select, patches, precision=highest)
    corr_east = correlate(east_shifted, east_patch, right_width)
    corr_south = correlate(south_shifted, south_patch, down_width)
    count = rows_here * cols_here * lax.axis_size("row") * lax.axis_size("col")
    square_sums = []
    west_rim = shifted_2(corr_east[:, :, cols_here - 1 : cols_here], "col", 1)
    north_rim = shifted_2(corr_south[:, rows_here - 1 : rows_here, :], "row", 1)
    corr_west = jnp.concatenate([west_rim, corr_east[:, :, :-1]], axis=2)
    corr_north = jnp.concatenate([north_rim, corr_south[:, :-1, :]], axis=1)
    phase_now = jnp.stack(
        [
            jnp.ones((rows_here, cols_here), jnp.float32),
            jnp.zeros((rows_here, cols_here), jnp.float32),
        ]
    )
    for step in range(ITERS):
        phase_now = apply_sync(phase_now, corr_east, corr_south, corr_west, corr_north)
        square_sums.append(jnp.sum(phase_now * phase_now))
    phase_now = phase_now * scale_last(square_sums, count)
    beside_all = neighbours(phase_now)
    east_phase = beside_all[0]
    south_phase = beside_all[1]
    east_place = jnp.einsum("pqkrd,pqcd->pqkrc", east_patch, east_select, precision=highest)
    south_place = jnp.einsum("pqab,pqkbc->pqkac", south_select, south_patch, precision=highest)
    own_factor = jnp.transpose(phase_now, (1, 2, 0))[:, :, :, None, None]
    east_factor = jnp.transpose(east_phase, (1, 2, 0))[:, :, :, None, None]
    south_factor = jnp.transpose(south_phase, (1, 2, 0))[:, :, :, None, None]
    numer = (
        rotate(own_factor, patches)
        + rotate(east_factor, east_place)
        + rotate(south_factor, south_place)
    )
    col_index = lax.axis_index("col") * cols_here + jnp.arange(cols_here, dtype=jnp.int32)
    row_index = lax.axis_index("row") * rows_here + jnp.arange(rows_here, dtype=jnp.int32)
    east_live = (col_index < cols_here * lax.axis_size("col") - 1)[None, :, None]
    south_live = (row_index < rows_here * lax.axis_size("row") - 1)[:, None, None]
    east_mask = (
        (lane_index >= right_offset[:, :, None])
        & (lane_index < right_offset[:, :, None] + right_width[:, :, None])
        & east_live
    ).astype(jnp.float32)
    south_mask = (
        (lane_index >= down_offset[:, :, None])
        & (lane_index < down_offset[:, :, None] + down_width[:, :, None])
        & south_live
    ).astype(jnp.float32)
    weight = 1.0 + east_mask[:, :, None, None, :] + south_mask[:, :, None, :, None]
    return (numer / weight, phase_now)


def solution(mesh):
    return jax.shard_map(
        local,
        mesh=mesh,
        in_specs=(
            P("row", "col", None, None, None),
            P("row", "col"),
            P("row", "col"),
            P("row", "col"),
            P("row", "col"),
        ),
        out_specs=(P("row", "col", None, None, None), P(None, "row", "col")),
        check_vma=False,
    )
```

profile of v0, /device:TPU:0, one launch (start us, length us, event | category | flops | bytes accessed | tf_op | source)
XLA Modules:
  0.0 197.4 jit_solution(5777450206083384091)
XLA Ops:
  0.7 1.4 collective-permute-start.2
  2.1 3.6 %collective-permute-start.1 = (f32[2,1,8]{2,1,0:T(1,128)}, f32[2,1,8]{2,1,0:T(1,128)}, u32[]{:S(2)}, u32[]{:S(2)}) collective-permute-start(f32[2,1,8]{2,1,0:T(1,128)} %constant.8.clone.1), channel_id=1, source_target_pairs={{0,8},{8,16},{16,24},{1,9},{9,17},{17,25},{2,10},{10,18},{18,26},{... | collective-permute-start | bytes 200 | tf_op jit(solution)/shard_map/ppermute | solution.py:20
  5.7 2.3 %slice.276 = f32[1,8,2,128,128]{4,3,2,1,0:T(8,128)} slice(f32[8,8,2,128,128]{4,3,2,1,0:T(8,128)} %param.5), slice={[0:1], [0:8], [0:2], [0:128], [0:128]} | slice | bytes 2097152 | tf_op jit(solution)/shard_map/slice | solution.py:96
  8.0 1.3 collective-permute-start.4
  9.6 1.3 collective-permute-start
  11.1 0.8 iota_add_fusion.1
  11.9 0.8 add.206
  12.8 12.5 %fusion.17 = f32[8,8,2,128,128]{4,3,2,1,0:T(8,128)} fusion(f32[8,8,2,128,128]{4,3,2,1,0:T(8,128)} %param.5, s32[8,8,128]{2,1,0:T(8,128)S(1)} %iota_add_fusion, pred[8,8,128]{2,1,0:T(8,128)(4,1)S(1)} %iota_compare_fusion.6), kind=kOutput, calls=%fused_computation.37 | convolution fusion | flops 3223322624 | bytes 16818176 | tf_op jit(solution)/shard_map/pqab,pqkac->pqkbc/dot_general | solution.py:108
  25.4 2.6 %broadcast_add_fusion = f32[8,8,128,128]{3,2,1,0:T(8,128)} fusion(f32[8,8,128]{2,1,0:T(8,128)S(1)} %fusion.36, f32[8,8,128]{2,1,0:T(8,128)S(1)} %convert_add_fusion), kind=kLoop, calls=%fused_computation.40 | loop fusion | flops 1048576 | bytes 4259840 | tf_op jit(solution)/shard_map/add | solution.py:154
  28.1 3.9 %slice.275 = f32[7,8,2,128,128]{4,3,2,1,0:T(8,128)} slice(f32[8,8,2,128,128]{4,3,2,1,0:T(8,128)S(1)} %bitcast.129), slice={[1:8], [0:8], [0:2], [0:128], [0:128]} | slice | bytes 14680064 | tf_op jit(solution)/shard_map/slice | solution.py:98
  32.0 4.0 %slice.266 = f32[8,7,2,128,128]{4,3,2,1,0:T(8,128)} slice(f32[8,8,2,128,128]{4,3,2,1,0:T(8,128)S(1)} %bitcast.129), slice={[0:8], [1:8], [0:2], [0:128], [0:128]} | slice | bytes 14680064 | tf_op jit(solution)/shard_map/slice | solution.py:97
  36.0 7.2 %convolution_bitcast_fusion = f32[8,8,2,128,128]{3,4,2,1,0:T(8,128)} fusion(f32[8,8,2,128,128]{4,3,2,1,0:T(8,128)S(1)} %bitcast.129, s32[8,8,128]{2,1,0:T(8,128)S(1)} %iota_add_fusion.1, pred[8,8,128]{2,1,0:T(8,128)(4,1)S(1)} %iota_compare_fusion.7), kind=kOutput, calls=%fused_computation.39 | convolution fusion | flops 3224371200 | bytes 16818176 | tf_op jit(solution)/shard_map/pqkrc,pqcd->pqkrd/dot_general | solution.py:107
  43.2 8.5 %copy.25 = f32[8,7,2,128,128]{3,4,2,1,0:T(8,128)} copy(f32[8,7,2,128,128]{4,3,2,1,0:T(8,128)} %slice.266) | data formatting | bytes 14680064
  51.7 0.6 pad_maximum_fusion.8
  52.3 0.7 fusion.78
  53.0 1.3 collective-permute-start.3
  54.3 6.7 %collective-permute-start.6 = (f32[2,10,1]{2,1,0:T(8,128)}, f32[2,10,1]{2,1,0:T(8,128)}, u32[]{:S(2)}, u32[]{:S(2)}) collective-permute-start(f32[2,10,1]{2,1,0:T(8,128)} %get-tuple-element.41), channel_id=1, source_target_pairs={{0,1},{1,2},{2,3},{3,4},{4,5},{5,6},{6,7},{8,9},{9,10},{10,11},{11... | collective-permute-start | bytes 248 | tf_op jit(solution)/shard_map/ppermute | solution.py:20
  61.0 8.5 %subtract_reduce_fusion = (f32[8,8]{1,0:T(8,128)S(1)}, f32[8,8]{1,0:T(8,128)S(1)}) fusion(f32[8,8,2,128,128]{4,3,2,1,0:T(8,128)} %fusion.17, f32[1,8,2,128,128]{4,3,2,1,0:T(8,128)S(1)} %collective-permute-done.4, f32[7,8,2,128,128]{4,3,2,1,0:T(8,128)} %slice.275), kind=kLoop, calls=%fused_computation.25 | loop fusion | flops 12582784 | bytes 16777728 | tf_op jit(solution)/shard_map/reduce_sum | solution.py:38
  69.6 1.2 copy-done
  70.8 5.2 %add_reduce_fusion.1 = (f32[8,8]{1,0:T(8,128)S(1)}, f32[8,8]{1,0:T(8,128)S(1)}) fusion(f32[8,8,2,128,128]{3,4,2,1,0:T(8,128)} %convolution_bitcast_fusion, f32[8,1,2,128,128]{3,4,2,1,0:T(8,128)S(1)} %collective-permute-done, f32[8,7,2,128,128]{3,4,2,1,0:T(8,128)S(1)} %copy-done), kind=kLoop, calls=%fused_computation.29 | loop fusion | flops 12582784 | bytes 16777728 | tf_op jit(solution)/shard_map/reduce_sum | solution.py:33
  76.0 0.6 fusion.57
  76.7 0.7 subtract_bitcast_fusion.2
  77.4 4.4 %collective-permute-start.5 = (f32[2,8,1]{2,1,0:T(8,128)S(1)}, f32[2,8,1]{2,1,0:T(8,128)S(1)}, u32[]{:S(2)}, u32[]{:S(2)}) collective-permute-start(f32[2,8,1]{2,1,0:T(8,128)S(1)} %slice_maximum_fusion), channel_id=1, source_target_pairs={{0,1},{1,2},{2,3},{3,4},{4,5},{5,6},{6,7},{8,9},{9,10},{10,11},{11... | collective-permute-start | bytes 200 | tf_op jit(solution)/shard_map/ppermute | solution.py:29
  81.9 2.6 %collective-permute-start.7 = (f32[2,1,8]{2,1,0:T(1,128)S(1)}, f32[2,1,8]{2,1,0:T(1,128)S(1)}, u32[]{:S(2)}, u32[]{:S(2)}) collective-permute-start(f32[2,1,8]{2,1,0:T(1,128)S(1)} %pad_maximum_fusion.36), channel_id=1, source_target_pairs={{0,8},{8,16},{16,24},{1,9},{9,17},{17,25},{2,10},{10,18},{18,26},{... | collective-permute-start | bytes 200 | tf_op jit(solution)/shard_map/ppermute | solution.py:29
  84.5 7.8 %fusion.20 = f32[8,8,2,128,128]{4,3,2,1,0:T(8,128)} fusion(f32[1,8,2,128,128]{4,3,2,1,0:T(8,128)S(1)} %collective-permute-done.4, f32[7,8,2,128,128]{4,3,2,1,0:T(8,128)S(1)} %bitcast.131, s32[8,8,128]{2,1,0:T(8,128)S(1)} %copy-done.5, pred[8,8,128]{2,1,0:T(8,128)(4,1)S(1)} %copy-done.11), kind=kOutput, calls=%fused_computation.38 | convolution fusion | flops 3225419776 | bytes 16818176 | tf_op jit(solution)/shard_map/pqab,pqkbc->pqkac/dot_general | solution.py:131
  92.4 0.8 multiply_add_fusion.5
  93.2 0.6 fusion.50
  93.9 0.6 multiply_reduce_fusion.1
  94.5 4.8 %collective-permute-start.8 = (f32[2,1,8]{2,1,0:T(1,128)S(1)}, f32[2,1,8]{2,1,0:T(1,128)S(1)}, u32[]{:S(2)}, u32[]{:S(2)}) collective-permute-start(f32[2,1,8]{2,1,0:T(1,128)S(1)} %get-tuple-element.55), channel_id=1, source_target_pairs={{0,8},{8,16},{16,24},{1,9},{9,17},{17,25},{2,10},{10,18},{18,26},{... | collective-permute-start | bytes 200 | tf_op jit(solution)/shard_map/ppermute | solution.py:20
  99.2 1.3 collective-permute-start.9
  100.5 1.7 collective-permute-done.9
  102.4 1.3 collective-permute-start.10
  103.7 4.5 %collective-permute-start.11 = (f32[2,10,1]{2,1,0:T(8,128)S(1)}, f32[2,10,1]{2,1,0:T(8,128)S(1)}, u32[]{:S(2)}, u32[]{:S(2)}) collective-permute-start(f32[2,10,1]{2,1,0:T(8,128)S(1)} %get-tuple-element.40), channel_id=1, source_target_pairs={{0,1},{1,2},{2,3},{3,4},{4,5},{5,6},{6,7},{8,9},{9,10},{10,11},{11... | collective-permute-start | bytes 248 | tf_op jit(solution)/shard_map/ppermute | solution.py:20
  108.4 1.3 collective-permute-done.11
  109.7 0.7 multiply_reduce_fusion
  110.4 1.3 pad_maximum_fusion.37
  111.8 9.5 %fusion.1 = f32[8,8,2,128,128]{4,3,2,1,0:T(8,128)} fusion(f32[8,1,2,128,128]{3,4,2,1,0:T(8,128)S(1)} %collective-permute-done, f32[8,7,2,128,128]{3,4,2,1,0:T(8,128)S(1)} %copy-done, s32[8,8,128]{2,1,0:T(8,128)S(1)} %copy-done.3, pred[8,8,128]{2,1,0:T(8,128)(4,1)S(1)} %copy-done.8), kind=kOutput, calls=%fused_computation.11 | convolution fusion | flops 3225419776 | bytes 16818176 | tf_op jit(solution)/shard_map/pqkrd,pqcd->pqkrc/dot_general | solution.py:130
  121.2 42.0 %psum.7 = f32[2]{0:T(128)S(1)} all-reduce(f32[2]{0:T(128)S(1)} %pad_maximum_fusion.37), channel_id=1, replica_groups=mesh['row'=4,'col'=8] {'row','col'}, use_global_device_ids=true, to_apply=%region_6.0 | all-reduce | flops 2 | bytes 16 | tf_op jit(solution)/shard_map/psum | solution.py:83
  163.2 0.6 fusion.81
  165.2 1.3 collective-permute-start.12
  166.5 1.3 collective-permute-start.13
  167.8 4.2 %collective-permute-done.13 = f32[2,1,8]{2,1,0:T(1,128)S(1)} collective-permute-done((f32[2,1,8]{2,1,0:T(1,128)S(1)}, f32[2,1,8]{2,1,0:T(1,128)S(1)}, u32[]{:S(2)}, u32[]{:S(2)}) %collective-permute-start.13) | collective-permute-done | bytes 96 | tf_op jit(solution)/shard_map/ppermute | solution.py:21
  172.1 1.5 collective-permute-start.14
  173.6 4.4 %multiply_subtract_fusion.2 = (f32[8,8,1,128,128]{4,3,2,1,0:T(8,128)S(1)}, f32[8,8,1,128,128]{4,3,2,1,0:T(8,128)S(1)}) fusion(f32[8,8,2,128,128]{4,3,2,1,0:T(8,128)} %param.5, f32[8,8]{1,0:T(8,128)S(1)} %get-tuple-element.53, f32[8,8]{1,0:T(8,128)S(1)} %get-tuple-element.52), kind=kLoop, calls=%fused_computation.24 | loop fusion | flops 6291456 | bytes 16777728 | tf_op jit(solution)/shard_map/sub | solution.py:61
  178.3 1.3 slice-done.8
  179.6 4.2 %multiply_subtract_fusion = (f32[8,8,1,128,128]{4,3,2,1,0:T(8,128)}, f32[8,8,1,128,128]{4,3,2,1,0:T(8,128)}) fusion(f32[8,8,2,128,128]{4,3,2,1,0:T(8,128)S(1)} %bitcast.135, f32[8,8]{1,0:T(8,128)S(1)} %get-tuple-element.47, f32[8,8]{1,0:T(8,128)S(1)} %get-tuple-element.46), kind=kLoop, calls=%fused_computation.20 | loop fusion | flops 6291456 | bytes 16777728 | tf_op jit(solution)/shard_map/sub | solution.py:61
  183.8 4.0 %multiply_subtract_fusion.1 = (f32[8,8,1,128,128]{4,3,2,1,0:T(8,128)}, f32[8,8,1,128,128]{4,3,2,1,0:T(8,128)}) fusion(f32[8,8,2,128,128]{4,3,2,1,0:T(8,128)S(1)} %bitcast.133, f32[8,8]{1,0:T(8,128)S(1)} %get-tuple-element.58, f32[8,8]{1,0:T(8,128)S(1)} %get-tuple-element.59), kind=kLoop, calls=%fused_computation.22 | loop fusion | flops 6291456 | bytes 16777728 | tf_op jit(solution)/shard_map/sub | solution.py:61
  187.9 9.6 %fusion.3 = f32[8,8,2,128,128]{4,3,2,1,0:T(8,128)} fusion(f32[8,8,1,128,128]{4,3,2,1,0:T(8,128)S(1)} %get-tuple-element.32, f32[8,8,1,128,128]{4,3,2,1,0:T(8,128)S(1)} %get-tuple-element.31, f32[8,8,1,128,128]{4,3,2,1,0:T(8,128)} %get-tuple-element.30, f32[8,8,1,128,128]{4,3,2,1,0:T(8,128)} %get-tuple-element.29, ...), kind=kLoop, calls=%fused_computation.14 | loop fusion | flops 12582912 | bytes 37748736 | tf_op jit(solution)/shard_map/div | solution.py:155
  (97 shorter events, 1.7 us)
Async XLA Ops:
  0.6 8.6 %slice-start.2 = ((f32[8,8,2,128,128]{4,3,2,1,0:T(8,128)}), f32[8,1,2,128,128]{4,3,2,1,0:T(8,128)S(1)}, s32[]{:S(2)}) async-start(f32[8,8,2,128,128]{4,3,2,1,0:T(8,128)} %param.5), calls=%async_computation.2 | async-start | bytes 2097152 | tf_op jit(solution)/shard_map/slice | solution.py:95
  0.6 10.3 %copy-start.15 = (s32[8,8]{1,0:T(8,128)S(1)}, s32[8,8]{1,0:T(8,128)}, u32[]{:S(2)}) copy-start(s32[8,8]{1,0:T(8,128)} %param.8) | copy-start | bytes 772
  0.7 10.3 %copy-start.12 = (s32[8,8]{1,0:T(8,128)S(1)}, s32[8,8]{1,0:T(8,128)}, u32[]{:S(2)}) copy-start(s32[8,8]{1,0:T(8,128)} %param.9) | copy-start | bytes 772
  0.7 11.2 %copy-start.13 = (s32[8,8]{1,0:T(8,128)S(1)}, s32[8,8]{1,0:T(8,128)}, u32[]{:S(2)}) copy-start(s32[8,8]{1,0:T(8,128)} %param.7) | copy-start | bytes 772
  0.7 51.0 %collective-permute-start.2 = (f32[2,1,8]{2,1,0:T(1,128)}, f32[2,1,8]{2,1,0:T(1,128)}, u32[]{:S(2)}, u32[]{:S(2)}) collective-permute-start(f32[2,1,8]{2,1,0:T(1,128)} %constant.8.clone.1), channel_id=1, source_target_pairs={{8,0},{16,8},{24,16},{9,1},{17,9},{25,17},{10,2},{18,10},{26,18},{... | collective-permute-start | bytes 200 | tf_op jit(solution)/shard_map/ppermute | solution.py:21
  2.1 49.6 %collective-permute-start.1 = (f32[2,1,8]{2,1,0:T(1,128)}, f32[2,1,8]{2,1,0:T(1,128)}, u32[]{:S(2)}, u32[]{:S(2)}) collective-permute-start(f32[2,1,8]{2,1,0:T(1,128)} %constant.8.clone.1), channel_id=1, source_target_pairs={{0,8},{8,16},{16,24},{1,9},{9,17},{17,25},{2,10},{10,18},{18,26},{... | collective-permute-start | bytes 200 | tf_op jit(solution)/shard_map/ppermute | solution.py:20
  8.0 53.1 %collective-permute-start.4 = (f32[1,8,2,128,128]{4,3,2,1,0:T(8,128)}, f32[1,8,2,128,128]{4,3,2,1,0:T(8,128)S(1)}, u32[]{:S(2)}, u32[]{:S(2)}) collective-permute-start(f32[1,8,2,128,128]{4,3,2,1,0:T(8,128)} %slice.276), channel_id=1, source_target_pairs={{8,0},{16,8},{24,16},{9,1},{17,9},{25,17},{10,2},{18,10},{26,18},{... | collective-permute-start | bytes 3145736 | tf_op jit(solution)/shard_map/ppermute | solution.py:29
  9.6 60.0 %collective-permute-start = (f32[8,1,2,128,128]{3,4,2,1,0:T(8,128)S(1)}, f32[8,1,2,128,128]{3,4,2,1,0:T(8,128)S(1)}, u32[]{:S(2)}, u32[]{:S(2)}) collective-permute-start(f32[8,1,2,128,128]{3,4,2,1,0:T(8,128)S(1)} %copy.26), channel_id=1, source_target_pairs={{1,0},{2,1},{3,2},{4,3},{5,4},{6,5},{7,6},{9,8},{10,9},{11,10},{12... | collective-permute-start | bytes 3145736 | tf_op jit(solution)/shard_map/ppermute | solution.py:29
  11.0 14.3 %copy-start.4 = (s32[8,8,128]{2,1,0:T(8,128)}, s32[8,8,128]{2,1,0:T(8,128)S(1)}, u32[]{:S(2)}) copy-start(s32[8,8,128]{2,1,0:T(8,128)S(1)} %iota_add_fusion) | copy-start | bytes 98308
  11.1 1.7 copy-start.10
  11.8 24.1 %copy-start.2 = (s32[8,8,128]{2,1,0:T(8,128)}, s32[8,8,128]{2,1,0:T(8,128)S(1)}, u32[]{:S(2)}) copy-start(s32[8,8,128]{2,1,0:T(8,128)S(1)} %iota_add_fusion.1) | copy-start | bytes 98308
  11.9 16.2 %slice-start = ((s8[8388608]{0:T(1024)(128)(4,1)}), s8[4194304]{0:T(1024)(128)(4,1)S(1)}, s32[]{:S(2)}) async-start(s8[8388608]{0:T(1024)(128)(4,1)} %bitcast.128), calls=%async_computation | async-start | bytes 8388608
  12.7 12.6 %copy-start.16 = (s32[8,8]{1,0:T(8,128)S(1)}, s32[8,8]{1,0:T(8,128)}, u32[]{:S(2)}) copy-start(s32[8,8]{1,0:T(8,128)} %param.6) | copy-start | bytes 772
  12.7 15.3 %slice-start.1 = ((s8[8388608]{0:T(1024)(128)(4,1)}), s8[4194304]{0:T(1024)(128)(4,1)S(1)}, s32[]{:S(2)}) async-start(s8[8388608]{0:T(1024)(128)(4,1)} %bitcast.128), calls=%async_computation.1 | async-start | bytes 8388608
  28.1 7.9 %copy-start.7 = (pred[8,8,128]{2,1,0:T(8,128)(4,1)}, pred[8,8,128]{2,1,0:T(8,128)(4,1)S(1)}, u32[]{:S(2)}) copy-start(pred[8,8,128]{2,1,0:T(8,128)(4,1)S(1)} %iota_compare_fusion.7) | copy-start | bytes 24580
  43.2 8.5 %copy-start.6 = (f32[2,8,8]{2,1,0:T(8,128)S(1)}, f32[2,8,8]{2,1,0:T(8,128)}, u32[]{:S(2)}) copy-start(f32[2,8,8]{2,1,0:T(8,128)} %constant.9.clone.1) | copy-start | bytes 1540
  53.0 23.6 %collective-permute-start.3 = (f32[2,10,1]{2,1,0:T(8,128)S(1)}, f32[2,10,1]{2,1,0:T(8,128)S(1)}, u32[]{:S(2)}, u32[]{:S(2)}) collective-permute-start(f32[2,10,1]{2,1,0:T(8,128)S(1)} %get-tuple-element.42), channel_id=1, source_target_pairs={{1,0},{2,1},{3,2},{4,3},{5,4},{6,5},{7,6},{9,8},{10,9},{11,10},{12... | collective-permute-start | bytes 248 | tf_op jit(solution)/shard_map/ppermute | solution.py:21
  54.3 38.1 %collective-permute-start.6 = (f32[2,10,1]{2,1,0:T(8,128)}, f32[2,10,1]{2,1,0:T(8,128)}, u32[]{:S(2)}, u32[]{:S(2)}) collective-permute-start(f32[2,10,1]{2,1,0:T(8,128)} %get-tuple-element.41), channel_id=1, source_target_pairs={{0,1},{1,2},{2,3},{3,4},{4,5},{5,6},{6,7},{8,9},{9,10},{10,11},{11... | collective-permute-start | bytes 248 | tf_op jit(solution)/shard_map/ppermute | solution.py:20
  61.0 9.7 %copy-start = (f32[8,7,2,128,128]{3,4,2,1,0:T(8,128)S(1)}, f32[8,7,2,128,128]{3,4,2,1,0:T(8,128)}, u32[]{:S(2)}) copy-start(f32[8,7,2,128,128]{3,4,2,1,0:T(8,128)} %copy.25) | copy-start | bytes 22020100
  61.0 23.4 %slice-start.3 = ((s8[7340032]{0:T(1024)(128)(4,1)}), s8[4194304]{0:T(1024)(128)(4,1)S(1)}, s32[]{:S(2)}) async-start(s8[7340032]{0:T(1024)(128)(4,1)} %bitcast.130), calls=%async_computation.3 | async-start | bytes 8388608
  69.6 7.1 %copy-start.14 = (s32[8,8]{1,0:T(8,128)S(1)}, s32[8,8]{1,0:T(8,128)}, u32[]{:S(2)}) copy-start(s32[8,8]{1,0:T(8,128)} %param.7) | copy-start | bytes 772
  69.6 14.9 %slice-start.4 = ((s8[7340032]{0:T(1024)(128)(4,1)}), s8[3145728]{0:T(1024)(128)(4,1)S(1)}, s32[]{:S(2)}) async-start(s8[7340032]{0:T(1024)(128)(4,1)} %bitcast.130), calls=%async_computation.4 | async-start | bytes 6291456
  70.8 13.7 %copy-start.5 = (s32[8,8,128]{2,1,0:T(8,128)S(1)}, s32[8,8,128]{2,1,0:T(8,128)}, u32[]{:S(2)}) copy-start(s32[8,8,128]{2,1,0:T(8,128)} %copy-done.4) | copy-start | bytes 98308
  70.8 13.7 %copy-start.11 = (pred[8,8,128]{2,1,0:T(8,128)(4,1)S(1)}, pred[8,8,128]{2,1,0:T(8,128)(4,1)}, u32[]{:S(2)}) copy-start(pred[8,8,128]{2,1,0:T(8,128)(4,1)} %copy-done.10) | copy-start | bytes 24580
  77.4 14.9 %collective-permute-start.5 = (f32[2,8,1]{2,1,0:T(8,128)S(1)}, f32[2,8,1]{2,1,0:T(8,128)S(1)}, u32[]{:S(2)}, u32[]{:S(2)}) collective-permute-start(f32[2,8,1]{2,1,0:T(8,128)S(1)} %slice_maximum_fusion), channel_id=1, source_target_pairs={{0,1},{1,2},{2,3},{3,4},{4,5},{5,6},{6,7},{8,9},{9,10},{10,11},{11... | collective-permute-start | bytes 200 | tf_op jit(solution)/shard_map/ppermute | solution.py:29
  81.9 29.9 %copy-start.3 = (s32[8,8,128]{2,1,0:T(8,128)S(1)}, s32[8,8,128]{2,1,0:T(8,128)}, u32[]{:S(2)}) copy-start(s32[8,8,128]{2,1,0:T(8,128)} %copy-done.2) | copy-start | bytes 98308
  81.9 29.9 %copy-start.8 = (pred[8,8,128]{2,1,0:T(8,128)(4,1)S(1)}, pred[8,8,128]{2,1,0:T(8,128)(4,1)}, u32[]{:S(2)}) copy-start(pred[8,8,128]{2,1,0:T(8,128)(4,1)} %copy-done.7) | copy-start | bytes 24580
  81.9 11.3 %collective-permute-start.7 = (f32[2,1,8]{2,1,0:T(1,128)S(1)}, f32[2,1,8]{2,1,0:T(1,128)S(1)}, u32[]{:S(2)}, u32[]{:S(2)}) collective-permute-start(f32[2,1,8]{2,1,0:T(1,128)S(1)} %pad_maximum_fusion.36), channel_id=1, source_target_pairs={{0,8},{8,16},{16,24},{1,9},{9,17},{17,25},{2,10},{10,18},{18,26},{... | collective-permute-start | bytes 200 | tf_op jit(solution)/shard_map/ppermute | solution.py:29
  94.5 6.1 %collective-permute-start.8 = (f32[2,1,8]{2,1,0:T(1,128)S(1)}, f32[2,1,8]{2,1,0:T(1,128)S(1)}, u32[]{:S(2)}, u32[]{:S(2)}) collective-permute-start(f32[2,1,8]{2,1,0:T(1,128)S(1)} %get-tuple-element.55), channel_id=1, source_target_pairs={{0,8},{8,16},{16,24},{1,9},{9,17},{17,25},{2,10},{10,18},{18,26},{... | collective-permute-start | bytes 200 | tf_op jit(solution)/shard_map/ppermute | solution.py:20
  99.2 3.1 %collective-permute-start.9 = (f32[2,1,8]{2,1,0:T(1,128)S(1)}, f32[2,1,8]{2,1,0:T(1,128)S(1)}, u32[]{:S(2)}, u32[]{:S(2)}) collective-permute-start(f32[2,1,8]{2,1,0:T(1,128)S(1)} %get-tuple-element.54), channel_id=1, source_target_pairs={{8,0},{16,8},{24,16},{9,1},{17,9},{25,17},{10,2},{18,10},{26,18},{... | collective-permute-start | bytes 200 | tf_op jit(solution)/shard_map/ppermute | solution.py:21
  102.4 5.9 %collective-permute-start.10 = (f32[2,10,1]{2,1,0:T(8,128)S(1)}, f32[2,10,1]{2,1,0:T(8,128)S(1)}, u32[]{:S(2)}, u32[]{:S(2)}) collective-permute-start(f32[2,10,1]{2,1,0:T(8,128)S(1)} %get-tuple-element.39), channel_id=1, source_target_pairs={{1,0},{2,1},{3,2},{4,3},{5,4},{6,5},{7,6},{9,8},{10,9},{11,10},{12... | collective-permute-start | bytes 248 | tf_op jit(solution)/shard_map/ppermute | solution.py:21
  103.7 6.0 %collective-permute-start.11 = (f32[2,10,1]{2,1,0:T(8,128)S(1)}, f32[2,10,1]{2,1,0:T(8,128)S(1)}, u32[]{:S(2)}, u32[]{:S(2)}) collective-permute-start(f32[2,10,1]{2,1,0:T(8,128)S(1)} %get-tuple-element.40), channel_id=1, source_target_pairs={{0,1},{1,2},{2,3},{3,4},{4,5},{5,6},{6,7},{8,9},{9,10},{10,11},{11... | collective-permute-start | bytes 248 | tf_op jit(solution)/shard_map/ppermute | solution.py:20
  165.2 12.8 %copy-start.9 = (f32[2,8,8]{2,1,0:T(8,128)}, f32[2,8,8]{2,1,0:T(8,128)S(1)}, u32[]{:S(2)}) copy-start(f32[2,8,8]{2,1,0:T(8,128)S(1)} %broadcast_multiply_fusion) | copy-start | bytes 1540
  165.2 2.6 %collective-permute-start.12 = (f32[2,1,8]{2,1,0:T(1,128)S(1)}, f32[2,1,8]{2,1,0:T(1,128)S(1)}, u32[]{:S(2)}, u32[]{:S(2)}) collective-permute-start(f32[2,1,8]{2,1,0:T(1,128)S(1)} %get-tuple-element.50), channel_id=1, source_target_pairs={{0,8},{8,16},{16,24},{1,9},{9,17},{17,25},{2,10},{10,18},{18,26},{... | collective-permute-start | bytes 200 | tf_op jit(solution)/shard_map/ppermute | solution.py:20
  166.5 5.6 %collective-permute-start.13 = (f32[2,1,8]{2,1,0:T(1,128)S(1)}, f32[2,1,8]{2,1,0:T(1,128)S(1)}, u32[]{:S(2)}, u32[]{:S(2)}) collective-permute-start(f32[2,1,8]{2,1,0:T(1,128)S(1)} %get-tuple-element.51), channel_id=1, source_target_pairs={{8,0},{16,8},{24,16},{9,1},{17,9},{25,17},{10,2},{18,10},{26,18},{... | collective-permute-start | bytes 200 | tf_op jit(solution)/shard_map/ppermute | solution.py:21
  172.1 5.9 %collective-permute-start.14 = (f32[2,10,1]{2,1,0:T(8,128)S(1)}, f32[2,10,1]{2,1,0:T(8,128)S(1)}, u32[]{:S(2)}, u32[]{:S(2)}) collective-permute-start(f32[2,10,1]{2,1,0:T(8,128)S(1)} %pad_maximum_fusion.6), channel_id=1, source_target_pairs={{1,0},{2,1},{3,2},{4,3},{5,4},{6,5},{7,6},{9,8},{10,9},{11,10},{12... | collective-permute-start | bytes 248 | tf_op jit(solution)/shard_map/ppermute | solution.py:21
  173.6 4.7 %slice-start.7 = ((s8[8388608]{0:T(1024)(128)(4,1)}), s8[4194304]{0:T(1024)(128)(4,1)S(1)}, s32[]{:S(2)}) async-start(s8[8388608]{0:T(1024)(128)(4,1)} %bitcast.134), calls=%async_computation.7 | async-start | bytes 8388608
  173.6 5.9 %slice-start.8 = ((s8[8388608]{0:T(1024)(128)(4,1)}), s8[4194304]{0:T(1024)(128)(4,1)S(1)}, s32[]{:S(2)}) async-start(s8[8388608]{0:T(1024)(128)(4,1)} %bitcast.134), calls=%async_computation.8 | async-start | bytes 8388608
  178.1 5.6 %slice-start.5 = ((s8[8388608]{0:T(1024)(128)(4,1)}), s8[4194304]{0:T(1024)(128)(4,1)S(1)}, s32[]{:S(2)}) async-start(s8[8388608]{0:T(1024)(128)(4,1)} %bitcast.132), calls=%async_computation.5 | async-start | bytes 8388608
  179.6 4.3 %slice-start.6 = ((s8[8388608]{0:T(1024)(128)(4,1)}), s8[4194304]{0:T(1024)(128)(4,1)S(1)}, s32[]{:S(2)}) async-start(s8[8388608]{0:T(1024)(128)(4,1)} %bitcast.132), calls=%async_computation.6 | async-start | bytes 8388608
  183.8 4.0 %copy-start.1 = (f32[8,8,128,128]{3,2,1,0:T(8,128)S(1)}, f32[8,8,128,128]{3,2,1,0:T(8,128)}, u32[]{:S(2)}) copy-start(f32[8,8,128,128]{3,2,1,0:T(8,128)} %broadcast_add_fusion) | copy-start | bytes 12582916
where the time goes:
time: 201 us; the launch traced here: 197 us
  other arithmetic  46.9 us (23%)
  blocking collectives  42 us (21%)
  starting transfers between devices  38.5 us (19%)
  matrix products  37 us (18%)
  local copies, waits for them, and re-layouts  23.2 us (12%)
  waiting for transfers between devices  7.31 us (4%)
  between operations  2.54 us (1%)
    psum x1, blocking collectives, scale_last(): totals = lax.psum(jnp.stack(square_sums), ('row', 'col'))  42 us
    ppermute x5, starting transfers between devices, extended(): before = lax.ppermute(last, axis, up)  20.9 us
    sub x3, other arithmetic, rotate(): factor[..., 0:1, :, :] * field[..., 0:1, :, :]  12.6 us
    dot_general x1, matrix products, local(): jnp.einsum('pqab,pqkac->pqkbc', south_select, patches, precision=highest)  12.5 us
    unnamed x52, local copies, waits for them, and re-layouts  11.7 us
    div x1, other arithmetic, local(): return (numer / weight, phase_now)  9.56 us
    ppermute x4, starting transfers between devices, shifted_2(): return lax.ppermute(array, axis, pairs)  9.55 us
    dot_general x1, matrix products, local(): jnp.einsum('pqkrd,pqcd->pqkrc', east_patch, east_select, precision=highest)  9.46 us
  transfers between devices with their start and end apart: 15, of which 3 were waited for; matrix products, arithmetic and copies ran while one was open for 37% of the time, Pallas kernels for 0%

commit v1 on v0

v1 whole, which is shorter than its diff:
```python
import functools

import jax
import jax.numpy as jnp
from jax import lax
from jax.experimental import pallas as pl
from jax.experimental.pallas import tpu as pltpu
from jax.sharding import PartitionSpec as P

ITERS = 2
PAD = 64
eps_norm = 1.0
highest = lax.Precision.HIGHEST
MESH = pl.DeviceIdType.MESH
f32 = jnp.float32


def fold_rows(x):
    return jnp.sum(x, axis=0, keepdims=True)


def pair_rows(a_re, a_im, b_re, b_im):
    return fold_rows(a_re * b_re + a_im * b_im), fold_rows(a_re * b_im - a_im * b_re)


def sync_kernel(
    dims, patches, ro, rw, do, dw, east_out, south_out, phase_out,
    pv, epack, east_recv, south_recv, acc, send_buf, recv, fields,
    col_sem, rest_sem, e_send, e_recv, s_send, s_recv, g_send, g_recv, out_sem,
):
    R, C, S, nr, nc = dims
    H, ndev = S // 2, nr * nc
    lo = H - 8
    span = S - lo
    my_row, my_col = lax.axis_index("row"), lax.axis_index("col")
    me = my_row * nc + my_col

    def coords(d):
        return (d // nc, d % nc)

    barrier = pltpu.get_barrier_semaphore()

    def greet(k, carry):
        pl.semaphore_signal(
            barrier, inc=1, device_id=coords(lax.rem(me + k, ndev)), device_id_type=MESH
        )
        return carry

    lax.fori_loop(1, ndev, greet, 0)

    cols = [
        pltpu.make_async_copy(
            patches.at[pl.ds(i * C * 2 * S, 2 * S)],
            pv.at[pl.ds(PAD + i * C * 2 * S, 2 * S)],
            col_sem.at[i],
        )
        for i in range(R)
    ]
    rests = [
        pltpu.make_async_copy(
            patches.at[pl.ds((i * C + 1) * 2 * S, (C - 1) * 2 * S)],
            pv.at[pl.ds(PAD + (i * C + 1) * 2 * S, (C - 1) * 2 * S)],
            rest_sem.at[i],
        )
        for i in range(R)
    ]
    for copy in cols:
        copy.start()
    for copy in rests:
        copy.start()
    for copy in cols:
        copy.wait()
    lane = lax.broadcasted_iota(jnp.int32, (S, S), 1)

    def pack(i, carry):
        base = pl.multiple_of(PAD + i * C * 2 * S, 8)
        re = pv[pl.ds(base, S), :]
        im = pv[pl.ds(base + S, S), :]
        epack[pl.ds(pl.multiple_of(i * S, 8), S), :] = jnp.where(
            lane < H, re, pltpu.roll(im, H, 1)
        )
        return carry

    lax.fori_loop(0, R, pack, 0)
    acc[...] = jnp.zeros_like(acc)
    pl.semaphore_wait(barrier, ndev - 1)

    def south_copy(k, row):
        return pltpu.make_async_remote_copy(
            src_ref=patches.at[pl.ds(k * S, H)],
            dst_ref=south_recv.at[pl.ds(PAD + k * H, H)],
            send_sem=s_send.at[k],
            recv_sem=s_recv.at[k],
            device_id=(row, my_col),
            device_id_type=MESH,
        )

    def east_copy(k, col):
        return pltpu.make_async_remote_copy(
            src_ref=epack.at[pl.ds(k * S, S)],
            dst_ref=east_recv.at[pl.ds(k * S, S)],
            send_sem=e_send.at[k],
            recv_sem=e_recv.at[k],
            device_id=(my_row, col),
            device_id_type=MESH,
        )

    @pl.when(my_col > 0)
    def _():
        for k in range(R):
            east_copy(k, my_col - 1).start()

    @pl.when(my_row > 0)
    def _():
        for k in range(2 * C):
            south_copy(k, my_row - 1).start()

    for copy in rests:
        copy.wait()

    lane1 = lax.broadcasted_iota(jnp.int32, (1, S), 1)
    rowid = lax.broadcasted_iota(jnp.int32, (span, S), 0) + lo

    def put(plane, p, re, im, width):
        scale = 1.0 / jnp.sqrt(jnp.full((1, S), S * width, jnp.int32).astype(f32))
        acc[pl.ds(plane * R * C + p, 1), :] = re * scale
        acc[pl.ds((plane + 1) * R * C + p, 1), :] = im * scale

    def east_store(i, j, b_re, b_im):
        p = i * C + j
        o, w = ro[i, j], rw[i, j]
        base = pl.multiple_of(PAD + p * 2 * S, 8)
        re, im = pair_rows(pv[pl.ds(base, S), :], pv[pl.ds(base + S, S), :], b_re, b_im)
        keep = (lane1 >= o) & (lane1 < o + w)
        put(0, p, jnp.where(keep, re, 0.0), jnp.where(keep, im, 0.0), w)

    def east_inner(n, carry):
        i, j = n // (C - 1), n % (C - 1)
        o = ro[i, j]
        base = pl.multiple_of(PAD + (i * C + j + 1) * 2 * S, 8)
        east_store(
            i, j,
            pltpu.roll(pv[pl.ds(base, S), :], o, 1),
            pltpu.roll(pv[pl.ds(base + S, S), :], o, 1),
        )
        return carry

    def south_store(i, j, b_re, b_im):
        p = i * C + j
        o, w = do[i, j], dw[i, j]
        base = pl.multiple_of(PAD + p * 2 * S + lo, 8)
        keep = (rowid >= o) & (rowid < o + w)
        re, im = pair_rows(
            pv[pl.ds(base, span), :],
            pv[pl.ds(base + S, span), :],
            jnp.where(keep, b_re, 0.0),
            jnp.where(keep, b_im, 0.0),
        )
        put(2, p, re, im, w)

    def south_inner(p, carry):
        i, j = p // C, p % C
        start = PAD + (p + C) * 2 * S + lo - do[i, j]
        south_store(i, j, pv[pl.ds(start, span), :], pv[pl.ds(start + S, span), :])
        return carry

    lax.fori_loop(0, R * (C - 1), east_inner, 0)
    lax.fori_loop(0, (R - 1) * C, south_inner, 0)

    @pl.when(my_row < nr - 1)
    def _():
        for k in range(2 * C):
            south_copy(k, my_row).wait_recv()

    @pl.when(my_row == nr - 1)
    def _():
        south_recv[...] = jnp.zeros_like(south_recv)

    south_back = pltpu.make_async_copy(
        south_recv.at[pl.ds(PAD, 2 * C * H)], south_out, out_sem.at[0]
    )
    south_back.start()

    def south_edge(j, carry):
        start = PAD + j * 2 * H + lo - do[R - 1, j]
        south_store(
            R - 1, j, south_recv[pl.ds(start, span), :], south_recv[pl.ds(start + H, span), :]
        )
        return carry

    lax.fori_loop(0, C, south_edge, 0)

    @pl.when(my_col < nc - 1)
    def _():
        for k in range(R):
            east_copy(k, my_col).wait_recv()

    @pl.when(my_col == nc - 1)
    def _():
        east_recv[...] = jnp.zeros_like(east_recv)

    east_back = pltpu.make_async_copy(east_recv, east_out, out_sem.at[1])
    east_back.start()

    def east_edge(i, carry):
        o = ro[i, C - 1]
        both = east_recv[pl.ds(pl.multiple_of(i * S, 8), S), :]
        east_store(i, C - 1, pltpu.roll(both, o, 1), pltpu.roll(both, lax.rem(o + H, S), 1))
        return carry

    lax.fori_loop(0, R, east_edge, 0)

    sums = lax.dot_general(
        jnp.ones((8, S), f32), acc[...], (((1,), (1,)), ((), ())),
        precision=highest, preferred_element_type=f32,
    )
    mine = jnp.concatenate([sums[0:1, :S], sums[0:1, S:]], axis=0)
    send_buf[...] = mine
    recv[me] = mine

    def gather_copy(target, source):
        return pltpu.make_async_remote_copy(
            src_ref=send_buf,
            dst_ref=recv.at[source],
            send_sem=g_send.at[target],
            recv_sem=g_recv.at[source],
            device_id=coords(target),
            device_id_type=MESH,
        )

    def spread(k, carry):
        gather_copy(lax.rem(me + k, ndev), me).start()
        return carry

    def collect(k, carry):
        other = lax.rem(me + k, ndev)
        gather_copy(other, other).wait_recv()
        return carry

    def drain(k, carry):
        gather_copy(lax.rem(me + k, ndev), me).wait_send()
        return carry

    lax.fori_loop(1, ndev, spread, 0)
    lax.fori_loop(1, ndev, collect, 0)

    got = recv[...]
    east, south = got[:, 0, :], got[:, 1, :]
    field = lax.broadcasted_iota(jnp.int32, (ndev, S), 0)
    slot = lax.broadcasted_iota(jnp.int32, (ndev, S), 1)
    valid = slot < R * C
    j_of, i_of = slot % C, (slot // C) % R
    dc, dr = field % nc, field // nc

    def roll(x, by, axis):
        return pltpu.roll(x, by % x.shape[axis], axis)

    def from_east(x):
        far = roll(roll(x, -1, 0), C - 1, 1)
        far = jnp.where(dc < nc - 1, far, 0.0)
        return jnp.where(j_of < C - 1, roll(x, -1, 1), far)

    def from_west(x):
        far = roll(roll(x, 1, 0), 1 - C, 1)
        far = jnp.where(dc > 0, far, 0.0)
        return jnp.where(j_of > 0, roll(x, 1, 1), far)

    def from_south(x):
        far = roll(roll(x, -nc, 0), (R - 1) * C, 1)
        far = jnp.where(dr < nr - 1, far, 0.0)
        return jnp.where(i_of < R - 1, roll(x, -C, 1), far)

    def from_north(x):
        far = roll(roll(x, nc, 0), -(R - 1) * C, 1)
        far = jnp.where(dr > 0, far, 0.0)
        return jnp.where(i_of > 0, roll(x, C, 1), far)

    ce = (jnp.where(valid, east, 0.0), jnp.where(valid, roll(east, -R * C, 1), 0.0))
    cs = (jnp.where(valid, south, 0.0), jnp.where(valid, roll(south, -R * C, 1), 0.0))
    cw = tuple(from_west(x) for x in ce)
    cn = tuple(from_north(x) for x in cs)
    count = float(ndev * R * C)

    def times(a, b):
        return (a[0] * b[0] - a[1] * b[1], a[0] * b[1] + a[1] * b[0])

    def conj_times(a, b):
        return (a[0] * b[0] + a[1] * b[1], a[0] * b[1] - a[1] * b[0])

    now = (jnp.ones((ndev, S), f32), jnp.zeros((ndev, S), f32))
    for step in range(ITERS):
        terms = (
            times(ce, tuple(from_east(x) for x in now)),
            times(cs, tuple(from_south(x) for x in now)),
            conj_times(cw, tuple(from_west(x) for x in now)),
            conj_times(cn, tuple(from_north(x) for x in now)),
        )
        image = tuple(
            jnp.where(valid, terms[0][q] + terms[1][q] + terms[2][q] + terms[3][q], 0.0)
            for q in range(2)
        )
        total = jnp.sum(image[0] * image[0] + image[1] * image[1], axis=0, keepdims=True)
        total = jnp.sum(total, axis=1, keepdims=True)
        factor = 1.0 / jnp.sqrt(total / count + eps_norm)
        now = (image[0] * factor, image[1] * factor)
    outs = now + tuple(from_east(x) for x in now) + tuple(from_south(x) for x in now)
    for q in range(6):
        fields[q] = outs[q]
    for q in range(6):
        phase_out[q : q + 1, :] = fields[q, pl.ds(me, 1), :]
    phase_out[6:8, :] = jnp.zeros((2, S), f32)

    lax.fori_loop(1, ndev, drain, 0)

    @pl.when(my_col > 0)
    def _():
        for k in range(R):
            east_copy(k, my_col - 1).wait_send()

    @pl.when(my_row > 0)
    def _():
        for k in range(2 * C):
            south_copy(k, my_row - 1).wait_send()

    south_back.wait()
    east_back.wait()


def blend_kernel(
    dims, patches, east_halo, south_halo, ro, rw, do, dw, g, out, phases,
    pv, ev, sv, ov, in_sem, halo_sem, out_sem,
):
    R, C, S, nr, nc = dims
    H = S // 2
    lo = H - 8
    span = S - lo
    row_size = C * 2 * S
    last_col = lax.axis_index("col") == nc - 1
    last_row = lax.axis_index("row") == nr - 1

    def load(i):
        return pltpu.make_async_copy(
            patches.at[pl.ds(i * row_size, row_size)],
            pv.at[pl.ds(PAD + i * row_size, row_size)],
            in_sem.at[i],
        )

    def save(i):
        return pltpu.make_async_copy(
            ov.at[pl.ds(i * row_size, row_size)],
            out.at[pl.ds(i * row_size, row_size)],
            out_sem.at[i],
        )

    east_load = pltpu.make_async_copy(east_halo, ev, halo_sem.at[0])
    south_load = pltpu.make_async_copy(south_halo, sv.at[pl.ds(PAD, 2 * C * H)], halo_sem.at[1])
    load(0).start()
    east_load.start()
    for i in range(1, R):
        load(i).start()
    south_load.start()

    lane = lax.broadcasted_iota(jnp.int32, (1, S), 1)
    rowid = lax.broadcasted_iota(jnp.int32, (span, S), 0) + lo

    def place(i, j, e_re, e_im, s_re, s_im):
        p = i * C + j
        oe, we, os, ws = ro[i, j], rw[i, j], do[i, j], dw[i, j]
        g_re, g_im = g[0, p], g[1, p]
        ge_re, ge_im, gs_re, gs_im = g[2, p], g[3, p], g[4, p], g[5, p]
        phases[0, i, j] = g_re
        phases[1, i, j] = g_im
        base = pl.multiple_of(PAD + p * 2 * S, 8)
        to = pl.multiple_of(p * 2 * S, 8)
        keep_e = (lane >= oe) & (lane < oe + we)
        live_e = keep_e & jnp.logical_not((j == C - 1) & last_col)
        fe_re = jnp.where(keep_e, ge_re, 0.0)
        fe_im = jnp.where(keep_e, ge_im, 0.0)
        a_re = pv[pl.ds(base, S), :]
        a_im = pv[pl.ds(base + S, S), :]
        n_re = (g_re * a_re - g_im * a_im) + (fe_re * e_re - fe_im * e_im)
        n_im = (g_re * a_im + g_im * a_re) + (fe_re * e_im + fe_im * e_re)
        half = jnp.where(live_e, f32(0.5), f32(1.0))
        third = jnp.where(live_e, f32(1.0 / 3.0), f32(0.5))
        ov[pl.ds(to, lo), :] = n_re[:lo] * half
        ov[pl.ds(pl.multiple_of(to + S, 8), lo), :] = n_im[:lo] * half
        keep_s = (rowid >= os) & (rowid < os + ws)
        p_re = gs_re * s_re - gs_im * s_im
        p_im = gs_re * s_im + gs_im * s_re
        down = jnp.logical_not((i == R - 1) & last_row)
        live_s = keep_s & down
        inv = jnp.where(live_s, third, half)
        ov[pl.ds(pl.multiple_of(to + lo, 8), span), :] = (
            n_re[lo:] + jnp.where(keep_s, p_re, 0.0)
        ) * inv
        ov[pl.ds(pl.multiple_of(to + S + lo, 8), span), :] = (
            n_im[lo:] + jnp.where(keep_s, p_im, 0.0)
        ) * inv

    def east_of(i, j):
        base = pl.multiple_of(PAD + (i * C + j + 1) * 2 * S, 8)
        o = ro[i, j]
        return pltpu.roll(pv[pl.ds(base, S), :], o, 1), pltpu.roll(pv[pl.ds(base + S, S), :], o, 1)

    def east_rim(i):
        o = ro[i, C - 1]
        both = ev[pl.ds(pl.multiple_of(i * S, 8), S), :]
        return pltpu.roll(both, o, 1), pltpu.roll(both, lax.rem(o + H, S), 1)

    def south_of(i, j):
        start = PAD + ((i + 1) * C + j) * 2 * S + lo - do[i, j]
        return pv[pl.ds(start, span), :], pv[pl.ds(start + S, span), :]

    def south_rim(j):
        start = PAD + j * 2 * H + lo - do[R - 1, j]
        return sv[pl.ds(start, span), :], sv[pl.ds(start + H, span), :]

    load(0).wait()
    east_load.wait()

    def rows(i, carry):
        load(i + 1).wait()

        def inner(j, c2):
            place(i, j, *east_of(i, j), *south_of(i, j))
            return c2

        lax.fori_loop(0, C - 1, inner, 0)
        place(i, C - 1, *east_rim(i), *south_of(i, C - 1))
        save(i).start()
        return carry

    lax.fori_loop(0, R - 1, rows, 0)
    south_load.wait()

    def last(j, c2):
        place(R - 1, j, *east_of(R - 1, j), *south_rim(j))
        return c2

    lax.fori_loop(0, C - 1, last, 0)
    place(R - 1, C - 1, *east_rim(R - 1), *south_rim(C - 1))
    save(R - 1).start()
    for i in range(R):
        save(i).wait()


def local(nr, nc, patches, right_offset, right_width, down_offset, down_width):
    R, C, _, S, _ = patches.shape
    H, ndev = S // 2, nr * nc
    dims = (R, C, S, nr, nc)
    flat = patches.reshape(R * C * 2 * S, S)
    anyspec = pl.BlockSpec(memory_space=pl.ANY)
    smem = pl.BlockSpec(memory_space=pltpu.SMEM)
    vmem = pl.BlockSpec(memory_space=pltpu.VMEM)
    dma = pltpu.SemaphoreType.DMA
    tables = (right_offset, right_width, down_offset, down_width)
    east_halo, south_halo, phase = pl.pallas_call(
        functools.partial(sync_kernel, dims),
        out_shape=(
            jax.ShapeDtypeStruct((R * S, S), f32),
            jax.ShapeDtypeStruct((2 * C * H, S), f32),
            jax.ShapeDtypeStruct((8, S), f32),
        ),
        in_specs=[anyspec] + [smem] * 4,
        out_specs=(anyspec, anyspec, vmem),
        scratch_shapes=[
            pltpu.VMEM((PAD + R * C * 2 * S, S), f32),
            pltpu.VMEM((R * S, S), f32),
            pltpu.VMEM((R * S, S), f32),
            pltpu.VMEM((2 * PAD + 2 * C * H, S), f32),
            pltpu.VMEM((4 * R * C, S), f32),
            pltpu.VMEM((2, S), f32),
            pltpu.VMEM((ndev, 2, S), f32),
            pltpu.VMEM((6, ndev, S), f32),
            dma((R,)), dma((R,)),
            dma((R,)), dma((R,)),
            dma((2 * C,)), dma((2 * C,)),
            dma((ndev,)), dma((ndev,)),
            dma((2,)),
        ],
        compiler_params=pltpu.CompilerParams(collective_id=0, has_side_effects=True),
        name="sync_patches",
    )(flat, *tables)
    blended, phases = pl.pallas_call(
        functools.partial(blend_kernel, dims),
        out_shape=(
            jax.ShapeDtypeStruct((R * C * 2 * S, S), f32),
            jax.ShapeDtypeStruct((2, R, C), f32),
        ),
        in_specs=[anyspec] * 3 + [smem] * 5,
        out_specs=(anyspec, smem),
        scratch_shapes=[
            pltpu.VMEM((PAD + R * C * 2 * S, S), f32),
            pltpu.VMEM((R * S, S), f32),
            pltpu.VMEM((2 * PAD + 2 * C * H, S), f32),
            pltpu.VMEM((R * C * 2 * S, S), f32),
            dma((R,)), dma((2,)), dma((R,)),
        ],
        name="blend_patches",
    )(flat, east_halo, south_halo, *tables, phase)
    return blended.reshape(patches.shape), phases


def solution(mesh):
    return jax.shard_map(
        functools.partial(local, mesh.shape["row"], mesh.shape["col"]),
        mesh=mesh,
        in_specs=(P("row", "col", None, None, None),) + (P("row", "col"),) * 4,
        out_specs=(P("row", "col", None, None, None), P(None, "row", "col")),
        check_vma=False,
    )
```

time: 201 us -> 42.3 us (0.21); the launches traced: 197 us -> 42 us
  other arithmetic: 46.9 us -> 0 us
  blocking collectives: 42 us -> 0 us
  Pallas kernels: 0 us -> 41.4 us
  starting transfers between devices: 38.5 us -> 0 us
  matrix products: 37 us -> 0 us
  local copies, waits for them, and re-layouts: 23.2 us -> 0 us
  waiting for transfers between devices: 7.31 us -> 0 us
    psum x1 -> x0, blocking collectives: 42 us -> none  [scale_last(): totals = lax.psum(jnp.stack(square_sums), ('row', 'col'))]
    pallas_call x0 -> x2, Pallas kernels: none -> 41.4 us  [the longest x1 28.7 us: local(): pl.pallas_call(functools.partial(sync_kernel, dims), out_shape=(jax.Shape...]
    ppermute x15 -> x0, starting transfers between devices: 38.5 us -> none  [the longest x5 20.9 us: extended(): before = lax.ppermute(last, axis, up)]
    dot_general x4 -> x0, matrix products: 37 us -> none  [the longest x1 12.5 us: local(): jnp.einsum('pqab,pqkac->pqkbc', south_select, patches, precision=highest)]
    reduce_sum x4 -> x0, other arithmetic: 15 us -> none  [the longest x1 8.53 us: correlate(): jnp.sum(shifted[..., 0, :, :] * partner[..., 1, :, :] - shifted[..., 1, :...]
    sub x5 -> x0, other arithmetic: 12.6 us -> none  [the longest x3 12.6 us: rotate(): factor[..., 0:1, :, :] * field[..., 0:1, :, :]]
    unnamed x52 -> x0, local copies, waits for them, and re-layouts: 11.7 us -> none
    slice x10 -> x0, local copies, waits for them, and re-layouts: 11.5 us -> none  [the longest x1 3.98 us: local(): east_patch = jnp.concatenate([patches[:, 1:], east_edge], axis=1)]
  transfers between devices with their start and end apart: 15 -> 0, of which waited for: 3 -> 0; matrix products, arithmetic and copies ran while one was open for 37% -> 0% of each run, Pallas kernels for 0% -> 0%
where the time goes in v1:
time: 42.3 us; the launch traced here: 42 us
  Pallas kernels  41.4 us (98%)
  between operations  0.64 us (2%)
    pallas_call x1, Pallas kernels, local(): pl.pallas_call(functools.partial(sync_kernel, dims), out_shape=(jax.Shape...  28.7 us
    pallas_call x1, Pallas kernels, local(): pl.pallas_call(functools.partial(blend_kernel, dims), out_shape=(jax.Shap...  12.7 us

profile of v1, /device:TPU:0, one launch (start us, length us, event | category | flops | bytes accessed | tf_op | source)
XLA Modules:
  0.0 42.0 jit_solution(17418404608500432152)
XLA Ops:
  0.6 28.7 %sync_patches.1 = (f32[1024,128]{1,0:T(8,128)}, f32[1024,128]{1,0:T(8,128)}, f32[8,128]{1,0:T(8,128)}) custom-call(f32[16384,128]{1,0:T(8,128)} %bitcast.2, s32[8,8]{1,0:T(8,128)} %ro.3, s32[8,8]{1,0:T(8,128)} %rw.3, s32[8,8]{1,0:T(8,128)} %do.3, s32[8,8]{1,0:T(8,128)} %dw.3), custom_call_target="tpu_custom_call" | custom-call | tf_op jit(solution)/shard_map/sync_patches/pallas_call | solution.py:457
  29.3 12.7 %blend_patches.1 = (f32[16384,128]{1,0:T(8,128)}, f32[2,8,8]{2,1,0:T(8,128)}) custom-call(f32[16384,128]{1,0:T(8,128)} %bitcast.3, f32[1024,128]{1,0:T(8,128)} %get-tuple-element.7.east_halo, f32[1024,128]{1,0:T(8,128)} %get-tuple-element.8.south_halo, s32[8,8]{1,0:T(8,128)} %ro.3, s32[8,8]{1,0:T(8,128)} %rw.3, s32[8,8]{1,0:T(8,128)} %do.3, s32[8,8]{1,0:T(8,128)} %dw.3, ...), custom_call_target="tpu_custom_call" | custom-call | tf_op jit(solution)/shard_map/blend_patches/pallas_call | solution.py:484

commit v2 on v1

--- a/solution.py
+++ b/solution.py
@@ -17,10 +17,6 @@
 
 def fold_rows(x):
     return jnp.sum(x, axis=0, keepdims=True)
-
-
-def pair_rows(a_re, a_im, b_re, b_im):
-    return fold_rows(a_re * b_re + a_im * b_im), fold_rows(a_re * b_im - a_im * b_re)
 
 
 def sync_kernel(
@@ -31,22 +27,15 @@
     R, C, S, nr, nc = dims
     H, ndev = S // 2, nr * nc
     lo = H - 8
-    span = S - lo
     my_row, my_col = lax.axis_index("row"), lax.axis_index("col")
     me = my_row * nc + my_col
 
-    def coords(d):
-        return (d // nc, d % nc)
-
+    turn_rows = [lax.rem(my_row + k, nr) for k in range(nr)]
+    turn_cols = [lax.rem(my_col + k, nc) for k in range(nc)]
+    others = [
+        (turn_rows[a], turn_cols[b]) for a in range(nr) for b in range(nc) if a or b
+    ]
     barrier = pltpu.get_barrier_semaphore()
-
-    def greet(k, carry):
-        pl.semaphore_signal(
-            barrier, inc=1, device_id=coords(lax.rem(me + k, ndev)), device_id_type=MESH
-        )
-        return carry
-
-    lax.fori_loop(1, ndev, greet, 0)
 
     cols = [
         pltpu.make_async_copy(
@@ -66,6 +55,8 @@
     ]
     for copy in cols:
         copy.start()
+    for other in others:
+        pl.semaphore_signal(barrier, inc=1, device_id=other, device_id_type=MESH)
     for copy in rests:
         copy.start()
     for copy in cols:
@@ -119,53 +110,71 @@
         copy.wait()
 
     lane1 = lax.broadcasted_iota(jnp.int32, (1, S), 1)
-    rowid = lax.broadcasted_iota(jnp.int32, (span, S), 0) + lo
+    row8 = lax.broadcasted_iota(jnp.int32, (8, S), 0)
 
     def put(plane, p, re, im, width):
         scale = 1.0 / jnp.sqrt(jnp.full((1, S), S * width, jnp.int32).astype(f32))
-        acc[pl.ds(plane * R * C + p, 1), :] = re * scale
-        acc[pl.ds((plane + 1) * R * C + p, 1), :] = im * scale
-
-    def east_store(i, j, b_re, b_im):
+        acc[pl.ds(plane * R * C + p, 1), :] = fold_rows(re) * scale
+        acc[pl.ds((plane + 1) * R * C + p, 1), :] = fold_rows(im) * scale
+
+    def gathered(pieces):
+        re, im = None, None
+        for a_re, a_im, b_re, b_im in pieces:
+            u, v = a_re * b_re + a_im * b_im, a_re * b_im - a_im * b_re
+            re, im = (u, v) if re is None else (re + u, im + v)
+        return re, im
+
+    def east_store(i, j, load_b):
         p = i * C + j
         o, w = ro[i, j], rw[i, j]
-        base = pl.multiple_of(PAD + p * 2 * S, 8)
-        re, im = pair_rows(pv[pl.ds(base, S), :], pv[pl.ds(base + S, S), :], b_re, b_im)
+        base = PAD + p * 2 * S
+        re, im = gathered(
+            (pv[pl.ds(pl.multiple_of(base + q, 8), 8), :],
+             pv[pl.ds(pl.multiple_of(base + S + q, 8), 8), :]) + load_b(q, o)
+            for q in range(0, S, 8)
+        )
         keep = (lane1 >= o) & (lane1 < o + w)
         put(0, p, jnp.where(keep, re, 0.0), jnp.where(keep, im, 0.0), w)
 
-    def east_inner(n, carry):
-        i, j = n // (C - 1), n % (C - 1)
-        o = ro[i, j]
-        base = pl.multiple_of(PAD + (i * C + j + 1) * 2 * S, 8)
-        east_store(
-            i, j,
-            pltpu.roll(pv[pl.ds(base, S), :], o, 1),
-            pltpu.roll(pv[pl.ds(base + S, S), :], o, 1),
-        )
+    def east_inner(i, carry):
+        for j in range(C - 1):
+            base = PAD + (i * C + j + 1) * 2 * S
+
+            def load_b(q, o):
+                return (
+                    pltpu.roll(pv[pl.ds(pl.multiple_of(base + q, 8), 8), :], o, 1),
+                    pltpu.roll(pv[pl.ds(pl.multiple_of(base + S + q, 8), 8), :], o, 1),
+                )
+
+            east_store(i, j, load_b)
         return carry
 
-    def south_store(i, j, b_re, b_im):
+    def south_store(i, j, ref, start, gap):
         p = i * C + j
         o, w = do[i, j], dw[i, j]
-        base = pl.multiple_of(PAD + p * 2 * S + lo, 8)
-        keep = (rowid >= o) & (rowid < o + w)
-        re, im = pair_rows(
-            pv[pl.ds(base, span), :],
-            pv[pl.ds(base + S, span), :],
-            jnp.where(keep, b_re, 0.0),
-            jnp.where(keep, b_im, 0.0),
-        )
+        base = PAD + p * 2 * S
+
+        def piece(q):
+            keep = row8 >= o - q if q < S - 8 else row8 < o + w - q
+            b_re = ref[pl.ds(start + (q - o), 8), :]
+            b_im = ref[pl.ds(start + gap + (q - o), 8), :]
+            return (
+                pv[pl.ds(pl.multiple_of(base + q, 8), 8), :],
+                pv[pl.ds(pl.multiple_of(base + S + q, 8), 8), :],
+                jnp.where(keep, b_re, 0.0),
+                jnp.where(keep, b_im, 0.0),
+            )
+
+        re, im = gathered(piece(q) for q in range(lo, S, 8))
         put(2, p, re, im, w)
 
-    def south_inner(p, carry):
-        i, j = p // C, p % C
-        start = PAD + (p + C) * 2 * S + lo - do[i, j]
-        south_store(i, j, pv[pl.ds(start, span), :], pv[pl.ds(start + S, span), :])
+    def south_inner(i, carry):
+        for j in range(C):
+            south_store(i, j, pv, PAD + ((i + 1) * C + j) * 2 * S, S)
         return carry
 
-    lax.fori_loop(0, R * (C - 1), east_inner, 0)
-    lax.fori_loop(0, (R - 1) * C, south_inner, 0)
+    lax.fori_loop(0, R, east_inner, 0)
+    lax.fori_loop(0, R - 1, south_inner, 0)
 
     @pl.when(my_row < nr - 1)
     def _():
@@ -181,34 +190,24 @@
     )
     south_back.start()
 
-    def south_edge(j, carry):
-        start = PAD + j * 2 * H + lo - do[R - 1, j]
-        south_store(
-            R - 1, j, south_recv[pl.ds(start, span), :], south_recv[pl.ds(start + H, span), :]
-        )
-        return carry
-
-    lax.fori_loop(0, C, south_edge, 0)
-
-    @pl.when(my_col < nc - 1)
-    def _():
-        for k in range(R):
-            east_copy(k, my_col).wait_recv()
+    for j in range(C):
+        south_store(R - 1, j, south_recv, PAD + j * 2 * H, H)
 
     @pl.when(my_col == nc - 1)
     def _():
         east_recv[...] = jnp.zeros_like(east_recv)
 
-    east_back = pltpu.make_async_copy(east_recv, east_out, out_sem.at[1])
-    east_back.start()
-
-    def east_edge(i, carry):
-        o = ro[i, C - 1]
-        both = east_recv[pl.ds(pl.multiple_of(i * S, 8), S), :]
-        east_store(i, C - 1, pltpu.roll(both, o, 1), pltpu.roll(both, lax.rem(o + H, S), 1))
-        return carry
-
-    lax.fori_loop(0, R, east_edge, 0)
+    for i in range(R):
+
+        @pl.when(my_col < nc - 1)
+        def _():
+            east_copy(i, my_col).wait_recv()
+
+        def load_b(q, o):
+            both = east_recv[pl.ds(i * S + q, 8), :]
+            return pltpu.roll(both, o, 1), pltpu.roll(both, lax.rem(o + H, S), 1)
+
+        east_store(i, C - 1, load_b)
 
     sums = lax.dot_general(
         jnp.ones((8, S), f32), acc[...], (((1,), (1,)), ((), ())),
@@ -218,31 +217,25 @@
     send_buf[...] = mine
     recv[me] = mine
 
+    def index(d):
+        return d[0] * nc + d[1]
+
     def gather_copy(target, source):
         return pltpu.make_async_remote_copy(
             src_ref=send_buf,
-            dst_ref=recv.at[source],
-            send_sem=g_send.at[target],
-            recv_sem=g_recv.at[source],
-            device_id=coords(target),
+            dst_ref=recv.at[index(source)],
+            send_sem=g_send.at[index(target)],
+            recv_sem=g_recv.at[index(source)],
+            device_id=target,
             device_id_type=MESH,
         )
 
-    def spread(k, carry):
-        gather_copy(lax.rem(me + k, ndev), me).start()
-        return carry
-
-    def collect(k, carry):
-        other = lax.rem(me + k, ndev)
+    for other in others:
+        gather_copy(other, (my_row, my_col)).start()
+    east_back = pltpu.make_async_copy(east_recv, east_out, out_sem.at[1])
+    east_back.start()
+    for other in others:
         gather_copy(other, other).wait_recv()
-        return carry
-
-    def drain(k, carry):
-        gather_copy(lax.rem(me + k, ndev), me).wait_send()
-        return carry
-
-    lax.fori_loop(1, ndev, spread, 0)
-    lax.fori_loop(1, ndev, collect, 0)
 
     got = recv[...]
     east, south = got[:, 0, :], got[:, 1, :]
@@ -310,7 +303,8 @@
         phase_out[q : q + 1, :] = fields[q, pl.ds(me, 1), :]
     phase_out[6:8, :] = jnp.zeros((2, S), f32)
 
-    lax.fori_loop(1, ndev, drain, 0)
+    for other in others:
+        gather_copy(other, (my_row, my_col)).wait_send()
 
     @pl.when(my_col > 0)
     def _():
@@ -333,7 +327,6 @@
     R, C, S, nr, nc = dims
     H = S // 2
     lo = H - 8
-    span = S - lo
     row_size = C * 2 * S
     last_col = lax.axis_index("col") == nc - 1
     last_row = lax.axis_index("row") == nr - 1
@@ -361,59 +354,68 @@
     south_load.start()
 
     lane = lax.broadcasted_iota(jnp.int32, (1, S), 1)
-    rowid = lax.broadcasted_iota(jnp.int32, (span, S), 0) + lo
-
-    def place(i, j, e_re, e_im, s_re, s_im):
+    row8 = lax.broadcasted_iota(jnp.int32, (8, S), 0)
+
+    def at(ref, row):
+        return ref[pl.ds(pl.multiple_of(row, 8), 8), :]
+
+    def place(i, j, east, ref, start, gap):
         p = i * C + j
         oe, we, os, ws = ro[i, j], rw[i, j], do[i, j], dw[i, j]
         g_re, g_im = g[0, p], g[1, p]
         ge_re, ge_im, gs_re, gs_im = g[2, p], g[3, p], g[4, p], g[5, p]
         phases[0, i, j] = g_re
         phases[1, i, j] = g_im
-        base = pl.multiple_of(PAD + p * 2 * S, 8)
-        to = pl.multiple_of(p * 2 * S, 8)
+        base = PAD + p * 2 * S
+        to = p * 2 * S
         keep_e = (lane >= oe) & (lane < oe + we)
         live_e = keep_e & jnp.logical_not((j == C - 1) & last_col)
-        fe_re = jnp.where(keep_e, ge_re, 0.0)
-        fe_im = jnp.where(keep_e, ge_im, 0.0)
-        a_re = pv[pl.ds(base, S), :]
-        a_im = pv[pl.ds(base + S, S), :]
-        n_re = (g_re * a_re - g_im * a_im) + (fe_re * e_re - fe_im * e_im)
-        n_im = (g_re * a_im + g_im * a_re) + (fe_re * e_im + fe_im * e_re)
         half = jnp.where(live_e, f32(0.5), f32(1.0))
         third = jnp.where(live_e, f32(1.0 / 3.0), f32(0.5))
-        ov[pl.ds(to, lo), :] = n_re[:lo] * half
-        ov[pl.ds(pl.multiple_of(to + S, 8), lo), :] = n_im[:lo] * half
-        keep_s = (rowid >= os) & (rowid < os + ws)
-        p_re = gs_re * s_re - gs_im * s_im
-        p_im = gs_re * s_im + gs_im * s_re
         down = jnp.logical_not((i == R - 1) & last_row)
-        live_s = keep_s & down
-        inv = jnp.where(live_s, third, half)
-        ov[pl.ds(pl.multiple_of(to + lo, 8), span), :] = (
-            n_re[lo:] + jnp.where(keep_s, p_re, 0.0)
-        ) * inv
-        ov[pl.ds(pl.multiple_of(to + S + lo, 8), span), :] = (
-            n_im[lo:] + jnp.where(keep_s, p_im, 0.0)
-        ) * inv
+        third = jnp.where(jnp.full((1, S), down), third, half)
+        half, third = jnp.broadcast_to(half, (8, S)), jnp.broadcast_to(third, (8, S))
+        e_re = jnp.broadcast_to(jnp.where(keep_e, ge_re, 0.0), (8, S))
+        e_im = jnp.broadcast_to(jnp.where(keep_e, ge_im, 0.0), (8, S))
+        h_re, h_im, x_re, x_im = g_re * half, g_im * half, e_re * half, e_im * half
+        for q in range(0, S, 8):
+            a_re, a_im = at(pv, base + q), at(pv, base + S + q)
+            b_re, b_im = east(q, oe)
+            if q < lo:
+                n_re = (h_re * a_re - h_im * a_im) + (x_re * b_re - x_im * b_im)
+                n_im = (h_re * a_im + h_im * a_re) + (x_re * b_im + x_im * b_re)
+            else:
+                keep = row8 >= os - q if q < S - 8 else row8 < os + ws - q
+                s_re = ref[pl.ds(start + (q - os), 8), :]
+                s_im = ref[pl.ds(start + gap + (q - os), 8), :]
+                n_re = (g_re * a_re - g_im * a_im) + (e_re * b_re - e_im * b_im)
+                n_im = (g_re * a_im + g_im * a_re) + (e_re * b_im + e_im * b_re)
+                inv = jnp.where(keep, third, half)
+                n_re = (n_re + jnp.where(keep, gs_re * s_re - gs_im * s_im, 0.0)) * inv
+                n_im = (n_im + jnp.where(keep, gs_re * s_im + gs_im * s_re, 0.0)) * inv
+            ov[pl.ds(pl.multiple_of(to + q, 8), 8), :] = n_re
+            ov[pl.ds(pl.multiple_of(to + S + q, 8), 8), :] = n_im
 
     def east_of(i, j):
-        base = pl.multiple_of(PAD + (i * C + j + 1) * 2 * S, 8)
-        o = ro[i, j]
-        return pltpu.roll(pv[pl.ds(base, S), :], o, 1), pltpu.roll(pv[pl.ds(base + S, S), :], o, 1)
+        base = PAD + (i * C + j + 1) * 2 * S
+
+        def east(q, o):
+            return pltpu.roll(at(pv, base + q), o, 1), pltpu.roll(at(pv, base + S + q), o, 1)
+
+        return east
 
     def east_rim(i):
-        o = ro[i, C - 1]
-        both = ev[pl.ds(pl.multiple_of(i * S, 8), S), :]
-        return pltpu.roll(both, o, 1), pltpu.roll(both, lax.rem(o + H, S), 1)
+        def east(q, o):
+            both = at(ev, i * S + q)
+            return pltpu.roll(both, o, 1), pltpu.roll(both, lax.rem(o + H, S), 1)
+
+        return east
 
     def south_of(i, j):
-        start = PAD + ((i + 1) * C + j) * 2 * S + lo - do[i, j]
-        return pv[pl.ds(start, span), :], pv[pl.ds(start + S, span), :]
+        return pv, PAD + ((i + 1) * C + j) * 2 * S, S
 
     def south_rim(j):
-        start = PAD + j * 2 * H + lo - do[R - 1, j]
-        return sv[pl.ds(start, span), :], sv[pl.ds(start + H, span), :]
+        return sv, PAD + j * 2 * H, H
 
     load(0).wait()
     east_load.wait()
@@ -422,11 +424,11 @@
         load(i + 1).wait()
 
         def inner(j, c2):
-            place(i, j, *east_of(i, j), *south_of(i, j))
+            place(i, j, east_of(i, j), *south_of(i, j))
             return c2
 
         lax.fori_loop(0, C - 1, inner, 0)
-        place(i, C - 1, *east_rim(i), *south_of(i, C - 1))
+        place(i, C - 1, east_rim(i), *south_of(i, C - 1))
         save(i).start()
         return carry
 
@@ -434,11 +436,11 @@
     south_load.wait()
 
     def last(j, c2):
-        place(R - 1, j, *east_of(R - 1, j), *south_rim(j))
+        place(R - 1, j, east_of(R - 1, j), *south_rim(j))
         return c2
 
     lax.fori_loop(0, C - 1, last, 0)
-    place(R - 1, C - 1, *east_rim(R - 1), *south_rim(C - 1))
+    place(R - 1, C - 1, east_rim(R - 1), *south_rim(C - 1))
     save(R - 1).start()
     for i in range(R):
         save(i).wait()

time: 42.3 us -> 40.3 us (0.953)
  Pallas kernels: 41.4 us -> 39.4 us
    pallas_call x1, Pallas kernels: 28.7 us -> 26.9 us  [local(): pl.pallas_call(functools.partial(sync_kernel, dims), out_shape=(jax.Shape...]
where the time goes in v2:
time: 40.3 us; the launch traced here: 40.1 us
  Pallas kernels  39.4 us (98%)
  between operations  0.64 us (2%)
    pallas_call x1, Pallas kernels, local(): pl.pallas_call(functools.partial(sync_kernel, dims), out_shape=(jax.Shape...  26.9 us
    pallas_call x1, Pallas kernels, local(): pl.pallas_call(functools.partial(blend_kernel, dims), out_shape=(jax.Shap...  12.5 us

profile of v2, /device:TPU:0, one launch (start us, length us, event | category | flops | bytes accessed | tf_op | source)
XLA Modules:
  0.0 40.1 jit_solution(13323292580436712367)
XLA Ops:
  0.6 26.9 %sync_patches.1 = (f32[1024,128]{1,0:T(8,128)}, f32[1024,128]{1,0:T(8,128)}, f32[8,128]{1,0:T(8,128)}) custom-call(f32[16384,128]{1,0:T(8,128)} %bitcast.2, s32[8,8]{1,0:T(8,128)} %ro.3, s32[8,8]{1,0:T(8,128)} %rw.3, s32[8,8]{1,0:T(8,128)} %do.3, s32[8,8]{1,0:T(8,128)} %dw.3), custom_call_target="tpu_custom_call" | custom-call | tf_op jit(solution)/shard_map/sync_patches/pallas_call | solution.py:459
  27.5 12.5 %blend_patches.1 = (f32[16384,128]{1,0:T(8,128)}, f32[2,8,8]{2,1,0:T(8,128)}) custom-call(f32[16384,128]{1,0:T(8,128)} %bitcast.3, f32[1024,128]{1,0:T(8,128)} %get-tuple-element.7.east_halo, f32[1024,128]{1,0:T(8,128)} %get-tuple-element.8.south_halo, s32[8,8]{1,0:T(8,128)} %ro.3, s32[8,8]{1,0:T(8,128)} %rw.3, s32[8,8]{1,0:T(8,128)} %do.3, s32[8,8]{1,0:T(8,128)} %dw.3, ...), custom_call_target="tpu_custom_call" | custom-call | tf_op jit(solution)/shard_map/blend_patches/pallas_call | solution.py:486

commit v3 on v2

--- a/solution.py
+++ b/solution.py
@@ -423,24 +423,16 @@
     def rows(i, carry):
         load(i + 1).wait()
 
-        def inner(j, c2):
-            place(i, j, east_of(i, j), *south_of(i, j))
-            return c2
-
-        lax.fori_loop(0, C - 1, inner, 0)
-        place(i, C - 1, east_rim(i), *south_of(i, C - 1))
+        for j in range(C):
+            place(i, j, east_of(i, j) if j < C - 1 else east_rim(i), *south_of(i, j))
         save(i).start()
         return carry
 
     lax.fori_loop(0, R - 1, rows, 0)
     south_load.wait()
 
-    def last(j, c2):
-        place(R - 1, j, east_of(R - 1, j), *south_rim(j))
-        return c2
-
-    lax.fori_loop(0, C - 1, last, 0)
-    place(R - 1, C - 1, east_rim(R - 1), *south_rim(C - 1))
+    for j in range(C):
+        place(R - 1, j, east_of(R - 1, j) if j < C - 1 else east_rim(R - 1), *south_rim(j))
     save(R - 1).start()
     for i in range(R):
         save(i).wait()

time: 40.3 us -> 37 us (0.918)
  Pallas kernels: 39.4 us -> 36.1 us
    pallas_call x1, Pallas kernels: 12.5 us -> 9.24 us  [local(): pl.pallas_call(functools.partial(blend_kernel, dims), out_shape=(jax.Shap...]
where the time goes in v3:
time: 37 us; the launch traced here: 36.8 us
  Pallas kernels  36.1 us (98%)
  between operations  0.64 us (2%)
    pallas_call x1, Pallas kernels, local(): pl.pallas_call(functools.partial(sync_kernel, dims), out_shape=(jax.Shape...  26.9 us
    pallas_call x1, Pallas kernels, local(): pl.pallas_call(functools.partial(blend_kernel, dims), out_shape=(jax.Shap...  9.24 us

profile of v3, /device:TPU:0, one launch (start us, length us, event | category | flops | bytes accessed | tf_op | source)
XLA Modules:
  0.0 36.8 jit_solution(15844009951398472001)
XLA Ops:
  0.6 26.9 %sync_patches.1 = (f32[1024,128]{1,0:T(8,128)}, f32[1024,128]{1,0:T(8,128)}, f32[8,128]{1,0:T(8,128)}) custom-call(f32[16384,128]{1,0:T(8,128)} %bitcast.2, s32[8,8]{1,0:T(8,128)} %ro.3, s32[8,8]{1,0:T(8,128)} %rw.3, s32[8,8]{1,0:T(8,128)} %do.3, s32[8,8]{1,0:T(8,128)} %dw.3), custom_call_target="tpu_custom_call" | custom-call | tf_op jit(solution)/shard_map/sync_patches/pallas_call | solution.py:451
  27.5 9.2 %blend_patches.1 = (f32[16384,128]{1,0:T(8,128)}, f32[2,8,8]{2,1,0:T(8,128)}) custom-call(f32[16384,128]{1,0:T(8,128)} %bitcast.3, f32[1024,128]{1,0:T(8,128)} %get-tuple-element.7.east_halo, f32[1024,128]{1,0:T(8,128)} %get-tuple-element.8.south_halo, s32[8,8]{1,0:T(8,128)} %ro.3, s32[8,8]{1,0:T(8,128)} %rw.3, s32[8,8]{1,0:T(8,128)} %do.3, s32[8,8]{1,0:T(8,128)} %dw.3, ...), custom_call_target="tpu_custom_call" | custom-call | tf_op jit(solution)/shard_map/blend_patches/pallas_call | solution.py:478

commit v4 on v3

--- a/solution.py
+++ b/solution.py
@@ -20,9 +20,9 @@
 
 
 def sync_kernel(
-    dims, patches, ro, rw, do, dw, east_out, south_out, phase_out,
-    pv, epack, east_recv, south_recv, acc, send_buf, recv, fields,
-    col_sem, rest_sem, e_send, e_recv, s_send, s_recv, g_send, g_recv, out_sem,
+    dims, patches, ro_in, rw_in, do_in, dw_in, pv, east_recv, south_recv, phase_out,
+    epack, acc, send_buf, recv, fields, ro, rw, do, dw,
+    col_sem, rest_sem, e_send, e_recv, s_send, s_recv, g_send, g_recv, table_sem,
 ):
     R, C, S, nr, nc = dims
     H, ndev = S // 2, nr * nc
@@ -53,28 +53,26 @@
         )
         for i in range(R)
     ]
+    tables = [
+        pltpu.make_async_copy(here, there, table_sem.at[k])
+        for k, (here, there) in enumerate(zip((ro_in, rw_in, do_in, dw_in), (ro, rw, do, dw)))
+    ]
     for copy in cols:
         copy.start()
     for other in others:
         pl.semaphore_signal(barrier, inc=1, device_id=other, device_id_type=MESH)
+    for copy in tables:
+        copy.start()
     for copy in rests:
         copy.start()
-    for copy in cols:
-        copy.wait()
     lane = lax.broadcasted_iota(jnp.int32, (S, S), 1)
 
-    def pack(i, carry):
-        base = pl.multiple_of(PAD + i * C * 2 * S, 8)
+    def pack(i):
+        base = PAD + i * C * 2 * S
+        cols[i].wait()
         re = pv[pl.ds(base, S), :]
         im = pv[pl.ds(base + S, S), :]
-        epack[pl.ds(pl.multiple_of(i * S, 8), S), :] = jnp.where(
-            lane < H, re, pltpu.roll(im, H, 1)
-        )
-        return carry
-
-    lax.fori_loop(0, R, pack, 0)
-    acc[...] = jnp.zeros_like(acc)
-    pl.semaphore_wait(barrier, ndev - 1)
+        epack[pl.ds(i * S, S), :] = jnp.where(lane < H, re, pltpu.roll(im, H, 1))
 
     def south_copy(k, row):
         return pltpu.make_async_remote_copy(
@@ -96,16 +94,28 @@
             device_id_type=MESH,
         )
 
-    @pl.when(my_col > 0)
-    def _():
-        for k in range(R):
-            east_copy(k, my_col - 1).start()
+    def send_east(i):
+        @pl.when(my_col > 0)
+        def _():
+            east_copy(i, my_col - 1).start()
+
+    for i in range(2):
+        pack(i)
+    pl.semaphore_wait(barrier, ndev - 1)
+    for i in range(2):
+        send_east(i)
 
     @pl.when(my_row > 0)
     def _():
         for k in range(2 * C):
             south_copy(k, my_row - 1).start()
 
+    for i in range(2, R):
+        pack(i)
+        send_east(i)
+    acc[...] = jnp.zeros_like(acc)
+    for copy in tables:
+        copy.wait()
     for copy in rests:
         copy.wait()
 
@@ -185,11 +195,6 @@
     def _():
         south_recv[...] = jnp.zeros_like(south_recv)
 
-    south_back = pltpu.make_async_copy(
-        south_recv.at[pl.ds(PAD, 2 * C * H)], south_out, out_sem.at[0]
-    )
-    south_back.start()
-
     for j in range(C):
         south_store(R - 1, j, south_recv, PAD + j * 2 * H, H)
 
@@ -232,8 +237,6 @@
 
     for other in others:
         gather_copy(other, (my_row, my_col)).start()
-    east_back = pltpu.make_async_copy(east_recv, east_out, out_sem.at[1])
-    east_back.start()
     for other in others:
         gather_copy(other, other).wait_recv()
 
@@ -316,13 +319,9 @@
         for k in range(2 * C):
             south_copy(k, my_row - 1).wait_send()
 
-    south_back.wait()
-    east_back.wait()
-
 
 def blend_kernel(
-    dims, patches, east_halo, south_halo, ro, rw, do, dw, g, out, phases,
-    pv, ev, sv, ov, in_sem, halo_sem, out_sem,
+    dims, pv, ev, sv, ro, rw, do, dw, g, out, phases, ov, out_sem,
 ):
     R, C, S, nr, nc = dims
     H = S // 2
@@ -331,27 +330,12 @@
     last_col = lax.axis_index("col") == nc - 1
     last_row = lax.axis_index("row") == nr - 1
 
-    def load(i):
-        return pltpu.make_async_copy(
-            patches.at[pl.ds(i * row_size, row_size)],
-            pv.at[pl.ds(PAD + i * row_size, row_size)],
-            in_sem.at[i],
-        )
-
     def save(i):
         return pltpu.make_async_copy(
             ov.at[pl.ds(i * row_size, row_size)],
             out.at[pl.ds(i * row_size, row_size)],
             out_sem.at[i],
         )
-
-    east_load = pltpu.make_async_copy(east_halo, ev, halo_sem.at[0])
-    south_load = pltpu.make_async_copy(south_halo, sv.at[pl.ds(PAD, 2 * C * H)], halo_sem.at[1])
-    load(0).start()
-    east_load.start()
-    for i in range(1, R):
-        load(i).start()
-    south_load.start()
 
     lane = lax.broadcasted_iota(jnp.int32, (1, S), 1)
     row8 = lax.broadcasted_iota(jnp.int32, (8, S), 0)
@@ -417,20 +401,13 @@
     def south_rim(j):
         return sv, PAD + j * 2 * H, H
 
-    load(0).wait()
-    east_load.wait()
-
     def rows(i, carry):
-        load(i + 1).wait()
-
         for j in range(C):
             place(i, j, east_of(i, j) if j < C - 1 else east_rim(i), *south_of(i, j))
         save(i).start()
         return carry
 
     lax.fori_loop(0, R - 1, rows, 0)
-    south_load.wait()
-
     for j in range(C):
         place(R - 1, j, east_of(R - 1, j) if j < C - 1 else east_rim(R - 1), *south_rim(j))
     save(R - 1).start()
@@ -448,50 +425,49 @@
     vmem = pl.BlockSpec(memory_space=pltpu.VMEM)
     dma = pltpu.SemaphoreType.DMA
     tables = (right_offset, right_width, down_offset, down_width)
-    east_halo, south_halo, phase = pl.pallas_call(
+    pv, east_halo, south_halo, phase = pl.pallas_call(
         functools.partial(sync_kernel, dims),
         out_shape=(
-            jax.ShapeDtypeStruct((R * S, S), f32),
-            jax.ShapeDtypeStruct((2 * C * H, S), f32),
+            pltpu.VMEM((PAD + R * C * 2 * S, S), f32),
+            pltpu.VMEM((R * S, S), f32),
+            pltpu.VMEM((2 * PAD + 2 * C * H, S), f32),
             jax.ShapeDtypeStruct((8, S), f32),
         ),
-        in_specs=[anyspec] + [smem] * 4,
-        out_specs=(anyspec, anyspec, vmem),
+        in_specs=[pl.BlockSpec(memory_space=pltpu.HBM)] * 5,
+        out_specs=(vmem,) * 4,
         scratch_shapes=[
-            pltpu.VMEM((PAD + R * C * 2 * S, S), f32),
             pltpu.VMEM((R * S, S), f32),
-            pltpu.VMEM((R * S, S), f32),
-            pltpu.VMEM((2 * PAD + 2 * C * H, S), f32),
             pltpu.VMEM((4 * R * C, S), f32),
             pltpu.VMEM((2, S), f32),
             pltpu.VMEM((ndev, 2, S), f32),
             pltpu.VMEM((6, ndev, S), f32),
+        ] + [pltpu.SMEM((R, C), jnp.int32)] * 4 + [
             dma((R,)), dma((R,)),
             dma((R,)), dma((R,)),
             dma((2 * C,)), dma((2 * C,)),
             dma((ndev,)), dma((ndev,)),
-            dma((2,)),
+            dma((4,)),
         ],
-        compiler_params=pltpu.CompilerParams(collective_id=0, has_side_effects=True),
+        compiler_params=pltpu.CompilerParams(
+            collective_id=0, has_side_effects=True, vmem_limit_bytes=16 << 20
+        ),
         name="sync_patches",
-    )(flat, *tables)
+    )(*(pltpu.with_memory_space_constraint(x, pltpu.HBM) for x in (flat, *tables)))
     blended, phases = pl.pallas_call(
         functools.partial(blend_kernel, dims),
         out_shape=(
             jax.ShapeDtypeStruct((R * C * 2 * S, S), f32),
             jax.ShapeDtypeStruct((2, R, C), f32),
         ),
-        in_specs=[anyspec] * 3 + [smem] * 5,
+        in_specs=[vmem] * 3 + [smem] * 5,
         out_specs=(anyspec, smem),
         scratch_shapes=[
-            pltpu.VMEM((PAD + R * C * 2 * S, S), f32),
-            pltpu.VMEM((R * S, S), f32),
-            pltpu.VMEM((2 * PAD + 2 * C * H, S), f32),
             pltpu.VMEM((R * C * 2 * S, S), f32),
-            dma((R,)), dma((2,)), dma((R,)),
+            dma((R,)),
         ],
+        compiler_params=pltpu.CompilerParams(vmem_limit_bytes=24 << 20),
         name="blend_patches",
-    )(flat, east_halo, south_halo, *tables, phase)
+    )(pv, east_halo, south_halo, *tables, phase)
     return blended.reshape(patches.shape), phases
 
 

time: 37 us -> 32.4 us (0.88)
  Pallas kernels: 36.1 us -> 31.5 us
    pallas_call x1, Pallas kernels: 9.24 us -> 6.22 us  [local(): pl.pallas_call(functools.partial(blend_kernel, dims), out_shape=(jax.Shap...]
    pallas_call x1, Pallas kernels: 26.9 us -> 25.3 us  [local(): pl.pallas_call(functools.partial(sync_kernel, dims), out_shape=(pltpu.VME...]
where the time goes in v4:
time: 32.4 us; the launch traced here: 32.3 us
  Pallas kernels  31.5 us (97%)
  between operations  0.7 us (2%)
    pallas_call x1, Pallas kernels, local(): pl.pallas_call(functools.partial(sync_kernel, dims), out_shape=(pltpu.VME...  25.3 us
    pallas_call x1, Pallas kernels, local(): pl.pallas_call(functools.partial(blend_kernel, dims), out_shape=(jax.Shap...  6.22 us

profile of v4, /device:TPU:0, one launch (start us, length us, event | category | flops | bytes accessed | tf_op | source)
XLA Modules:
  0.0 32.3 jit_solution(8461803743883005400)
XLA Ops:
  0.6 0.0 copy-start.3
  0.6 0.0 copy-start.2
  0.7 0.0 copy-start.1
  0.7 0.0 copy-start
  0.7 25.3 %sync_patches.1 = (f32[16448,128]{1,0:T(8,128)S(1)}, f32[1024,128]{1,0:T(8,128)S(1)}, f32[1152,128]{1,0:T(8,128)S(1)}, f32[8,128]{1,0:T(8,128)S(1)}) custom-call(f32[16384,128]{1,0:T(8,128)} %bitcast.2, s32[8,8]{1,0:T(8,128)} %ro.1, s32[8,8]{1,0:T(8,128)} %rw.1, s32[8,8]{1,0:T(8,128)} %do.1, s32[8,8]{1,0:T(8,128)} %dw.1), custom_call_target="tpu_custom_call" | custom-call | tf_op jit(solution)/shard_map/sync_patches/pallas_call | solution.py:428
  26.0 0.0 copy-done.3
  26.0 0.0 copy-done.2
  26.0 0.0 copy-done.1
  26.0 0.0 copy-done
  26.0 6.2 %blend_patches.1 = (f32[16384,128]{1,0:T(8,128)}, f32[2,8,8]{2,1,0:T(8,128)}) custom-call(f32[16448,128]{1,0:T(8,128)S(1)} %get-tuple-element.8.pv, f32[1024,128]{1,0:T(8,128)S(1)} %get-tuple-element.9.ev, f32[1152,128]{1,0:T(8,128)S(1)} %get-tuple-element.10.sv, s32[8,8]{1,0:T(8,128)S(1)} %copy-done, s32[8,8]{1,0:T(8,128)S(1)} %copy-done.1, ...), custom_call_target="tpu_custom_call" | custom-call | tf_op jit(solution)/shard_map/blend_patches/pallas_call | solution.py:456
Async XLA Ops:
  0.6 25.4 %copy-start.3 = (s32[8,8]{1,0:T(8,128)S(1)}, s32[8,8]{1,0:T(8,128)}, u32[]{:S(2)}) copy-start(s32[8,8]{1,0:T(8,128)} %dw.1) | copy-start | bytes 772
  0.6 25.4 %copy-start.2 = (s32[8,8]{1,0:T(8,128)S(1)}, s32[8,8]{1,0:T(8,128)}, u32[]{:S(2)}) copy-start(s32[8,8]{1,0:T(8,128)} %do.1) | copy-start | bytes 772
  0.7 25.4 %copy-start.1 = (s32[8,8]{1,0:T(8,128)S(1)}, s32[8,8]{1,0:T(8,128)}, u32[]{:S(2)}) copy-start(s32[8,8]{1,0:T(8,128)} %rw.1) | copy-start | bytes 772
  0.7 25.4 %copy-start = (s32[8,8]{1,0:T(8,128)S(1)}, s32[8,8]{1,0:T(8,128)}, u32[]{:S(2)}) copy-start(s32[8,8]{1,0:T(8,128)} %ro.1) | copy-start | bytes 772
